TPU v7x, 32 devices: a whole 2x2x4 slice. The times are simulated.
32 devices in a mesh: fsdp: 4 (over z), context: 2 (over y), tensor: 4 (over x, core).
Axes of the slice: x: 2, y: 2, z: 4, core: 2. Of those that a mesh axis runs over, the one named last changes fastest.
Arguments:
- hidden_in: bfloat16 [4, 1024, 2048], P('fsdp', 'context'), may hold values from -6 to 6
- attn_gain: bfloat16 [2048], P(('fsdp', 'context')), may hold values from 0.5 to 1.5
- w_query: bfloat16 [2048, 4096], P(('fsdp', 'context'), 'tensor'), may hold values from -0.125 to 0.125
- key_weight: bfloat16 [2048, 512], P(('fsdp', 'context'), 'tensor'), may hold values from -0.125 to 0.125
- value_weight: bfloat16 [2048, 512], P(('fsdp', 'context'), 'tensor'), may hold values from -0.125 to 0.125
- w_output: bfloat16 [2048, 4096], P(('fsdp', 'context'), 'tensor'), may hold values from -0.5 to 0.5
- query_gain: bfloat16 [128], P(('fsdp', 'context')), may hold values from 0.796875 to 2
- key_gain: bfloat16 [128], P(('fsdp', 'context')), may hold values from 0.796875 to 2
- ffn_gain: bfloat16 [2048], P(('fsdp', 'context')), may hold values from 0.5 to 1.5
- router: bfloat16 [2048, 32], P(('fsdp', 'context')), may hold values from -0.0625 to 0.0625
- gate_weight: bfloat16 [32, 2048, 768], P(('fsdp', 'context'), None, 'tensor'), may hold values from -0.125 to 0.125
- up_weight: bfloat16 [32, 2048, 768], P(('fsdp', 'context'), None, 'tensor'), may hold values from -0.125 to 0.125
- down_weight: bfloat16 [32, 768, 2048], P(('fsdp', 'context'), 'tensor'), may hold values from -1.25 to 1.25
- routes: int32 [4, 1024, 8], P('fsdp', 'context'), may hold values from 0 to 31, all different within a row
- segments: int32 [4, 1024], P('fsdp', 'context'), may hold values from 0 to 3, never falling along the last dimension, each value on 1 to 512 neighbouring positions
- cotangent: bfloat16 [4, 1024, 2048], P('fsdp', 'context'), may hold values from -6 to 6
Outputs:
- output: bfloat16 [4, 1024, 2048], P('fsdp', 'context')
- input_grad: float32 [4, 1024, 2048], P('fsdp', 'context')
- grad_attn_gain: float32 [2048], P(('fsdp', 'context'))
- grad_w_query: float32 [2048, 4096], P(('fsdp', 'context'), 'tensor')
- grad_w_key: float32 [2048, 512], P(('fsdp', 'context'), 'tensor')
- grad_w_value: float32 [2048, 512], P(('fsdp', 'context'), 'tensor')
- grad_w_output: float32 [2048, 4096], P(('fsdp', 'context'), 'tensor')
- grad_query_gain: float32 [128], P(('fsdp', 'context'))
- grad_key_gain: float32 [128], P(('fsdp', 'context'))
- grad_ffn_gain: float32 [2048], P(('fsdp', 'context'))
- grad_router: float32 [2048, 32], P(('fsdp', 'context'))
- grad_w_gate: float32 [32, 2048, 768], P(('fsdp', 'context'), None, 'tensor')
- grad_w_up: float32 [32, 2048, 768], P(('fsdp', 'context'), None, 'tensor')
- grad_w_down: float32 [32, 768, 2048], P(('fsdp', 'context'), 'tensor')
Inputs may be any that keep to these rules, and one draw needn't show every extreme that they name: `routes`: the 8 experts of a token are different. `segments`: segment numbers never fall along a sequence.
All inputs are finite; a program needn't handle non-finite values.
Results may differ from a plain program's by a relative error of at most 0.03.
Values may be sent and summed in bfloat16 or wider, within the bound.
A program may use at most 320 MiB of HBM per device.

v0:
```python
import functools
import math

import jax
import jax.numpy as jnp
from jax import lax
from jax.experimental import pallas as pl
from jax.experimental.pallas import tpu as pltpu
from jax.sharding import PartitionSpec as P

HEAD_SIZE = 128
TOPK = 8
FSDP, CONTEXT, TENSOR = "fsdp", "context", "tensor"
GROUPS = (FSDP, CONTEXT)
EVERYONE = (FSDP, CONTEXT, TENSOR)


EPSILON = 1e-06
ROPE_BASE = 1000000.0
NEGATIVE = -1e30


def rms_scale(values, gain_vec):
    return (
        values * lax.rsqrt(jnp.mean(values * values, axis=-1, keepdims=True) + EPSILON) * gain_vec
    )


def rotate(values):
    half_width = values.shape[-1] // 2
    return jnp.concatenate([-values[..., half_width:], values[..., :half_width]], axis=-1)


def rope_tables(positions, head_width):
    step_index = jnp.arange(head_width // 2, dtype=jnp.float32)
    inverse = jnp.exp(step_index * (-2.0 * math.log(ROPE_BASE) / head_width))
    angles = positions.astype(jnp.float32)[:, None] * inverse[None, :]
    cosine_table = jnp.cos(angles)
    sine_table = jnp.sin(angles)
    return (
        jnp.concatenate([cosine_table, cosine_table], -1),
        jnp.concatenate([sine_table, sine_table], -1),
    )


def doc_positions(segment):
    token_index = jnp.arange(segment.shape[0], dtype=jnp.int32)
    smaller = (segment[None, :] < segment[:, None]).astype(jnp.int32)
    return token_index - jnp.sum(smaller, axis=1)


def earlier_counts(chosen):
    rows = chosen.shape[0]
    row_id = lax.broadcasted_iota(jnp.int32, (rows, rows), 0)
    col_id = lax.broadcasted_iota(jnp.int32, (rows, rows), 1)
    earlier = (col_id < row_id).astype(jnp.bfloat16)
    return matmul(earlier, chosen.astype(jnp.bfloat16))


def qk_finish(raw_values, gain_vec, cosine_table, sine_table):
    normed = rms_scale(raw_values, gain_vec)
    return normed * cosine_table + rotate(normed) * sine_table


def matmul(left_side, right_side):
    return jnp.dot(left_side, right_side, preferred_element_type=jnp.float32)


def matmul_nt(left_side, right_side):
    return lax.dot_general(
        left_side, right_side, (((1,), (1,)), ((), ())), preferred_element_type=jnp.float32
    )


def matmul_tn(left_side, right_side):
    return lax.dot_general(
        left_side, right_side, (((0,), (0,)), ((), ())), preferred_element_type=jnp.float32
    )


def block_scores(query_vectors, keys_all, seg_all, query_seg, query_index, key_ids, block_id, key_block):
    leading_row = block_id * key_block
    keys_part = lax.dynamic_slice_in_dim(keys_all, leading_row, key_block, 0)
    seg_part = lax.dynamic_slice_in_dim(seg_all, leading_row, key_block, 0)
    key_index = lax.dynamic_slice_in_dim(key_ids, leading_row, key_block, 0)
    score_scale = query_vectors.shape[2] ** (-0.5)
    scores = (
        jnp.einsum("qhd,kd->hqk", query_vectors, keys_part, preferred_element_type=jnp.float32)
        * score_scale
    )
    allowed = (query_seg[:, None] == seg_part[None, :]) & (
        key_index[None, :] <= query_index[:, None]
    )
    return (scores, allowed[None, :, :], keys_part)


def attention_forward(
    query_vectors, keys_all, values_all, seg_all, query_seg, query_index, key_ids, key_block
):
    row_count, head_count, head_width = query_vectors.shape
    block_count = keys_all.shape[0] // key_block

    def stats_step(running, block_id):
        run_max, run_sum = running
        scores, allowed, unused = block_scores(
            query_vectors, keys_all, seg_all, query_seg, query_index, key_ids, block_id, key_block
        )
        masked = jnp.where(allowed, scores, NEGATIVE)
        new_max = jnp.maximum(run_max, jnp.max(masked, axis=2))
        weights = jnp.where(allowed, jnp.exp(masked - new_max[:, :, None]), 0.0)
        run_sum = run_sum * jnp.exp(run_max - new_max) + jnp.sum(weights, axis=2)
        return ((new_max, run_sum), None)

    start_state = (
        jnp.full((head_count, row_count), NEGATIVE, jnp.float32),
        jnp.zeros((head_count, row_count), jnp.float32),
    )
    (run_max, run_sum), ignored = lax.scan(
        stats_step, start_state, jnp.arange(block_count, dtype=jnp.int32)
    )
    log_total = run_max + jnp.log(run_sum)

    def value_step(accumulated, block_id):
        scores, allowed, unused = block_scores(
            query_vectors, keys_all, seg_all, query_seg, query_index, key_ids, block_id, key_block
        )
        prob_block = jnp.where(allowed, jnp.exp(scores - log_total[:, :, None]), 0.0).astype(
            jnp.bfloat16
        )
        values_part = lax.dynamic_slice_in_dim(values_all, block_id * key_block, key_block, 0)
        accumulated = accumulated + jnp.einsum(
            "hqk,kd->qhd", prob_block, values_part, preferred_element_type=jnp.float32
        )
        return (accumulated, None)

    heads_full, ignored = lax.scan(
        value_step,
        jnp.zeros((row_count, head_count, head_width), jnp.float32),
        jnp.arange(block_count, dtype=jnp.int32),
    )
    return (heads_full, log_total)


def attention_backward(
    query_vectors,
    keys_all,
    values_all,
    seg_all,
    query_seg,
    query_index,
    key_ids,
    key_block,
    log_total,
    grad_heads,
    row_delta,
):
    row_count, head_count, head_width = query_vectors.shape
    block_count = keys_all.shape[0] // key_block
    score_scale = head_width ** (-0.5)

    def grad_step(grad_query, block_id):
        scores, allowed, keys_part = block_scores(
            query_vectors, keys_all, seg_all, query_seg, query_index, key_ids, block_id, key_block
        )
        values_part = lax.dynamic_slice_in_dim(values_all, block_id * key_block, key_block, 0)
        prob_block = jnp.where(allowed, jnp.exp(scores - log_total[:, :, None]), 0.0)
        grad_prob = jnp.einsum(
            "qhd,kd->hqk", grad_heads, values_part, preferred_element_type=jnp.float32
        )
        grad_score = (prob_block * (grad_prob - row_delta[:, :, None])).astype(jnp.bfloat16)
        grad_query = (
            grad_query
            + jnp.einsum("hqk,kd->qhd", grad_score, keys_part, preferred_element_type=jnp.float32)
            * score_scale
        )
        grad_key = (
            jnp.einsum("hqk,qhd->kd", grad_score, query_vectors, preferred_element_type=jnp.float32)
            * score_scale
        )
        grad_value = jnp.einsum(
            "hqk,qhd->kd",
            prob_block.astype(jnp.bfloat16),
            grad_heads,
            preferred_element_type=jnp.float32,
        )
        return (grad_query, (grad_key, grad_value))

    grad_query, (grad_key, grad_value) = lax.scan(
        grad_step,
        jnp.zeros((row_count, head_count, head_width), jnp.float32),
        jnp.arange(block_count, dtype=jnp.int32),
    )
    return (grad_query, grad_key.reshape(-1, head_width), grad_value.reshape(-1, head_width))


def to_experts(buffer):
    return lax.all_to_all(buffer, GROUPS, split_axis=0, concat_axis=1, tiled=True)


def from_experts(result_rows):
    return lax.all_to_all(result_rows, GROUPS, split_axis=1, concat_axis=0, tiled=True)


def pick_pairs(buffer, target, row_count):
    model_width = buffer.shape[2]
    flat_rows = jnp.concatenate(
        [buffer.reshape(-1, model_width), jnp.zeros((1, model_width), buffer.dtype)], axis=0
    )
    return flat_rows[target].reshape(row_count, TOPK, model_width)


def routed_local(
    hidden_in,
    attn_gain,
    w_query,
    key_weight,
    value_weight,
    w_output,
    query_gain,
    key_gain,
    ffn_gain,
    router,
    gate_weight,
    up_weight,
    down_weight,
    routes,
    segments,
    cotangent,
):
    context_rank = lax.axis_index(CONTEXT)
    input_rows = hidden_in[0].astype(jnp.float32)
    row_count, model_width = input_rows.shape
    gathered = (
        lax.all_gather(w_query, GROUPS, axis=0, tiled=True),
        lax.all_gather(key_weight, GROUPS, axis=0, tiled=True),
        lax.all_gather(value_weight, GROUPS, axis=0, tiled=True),
        lax.all_gather(w_output, GROUPS, axis=0, tiled=True),
        lax.all_gather(router, GROUPS, axis=0, tiled=True),
        lax.all_gather(attn_gain, GROUPS, axis=0, tiled=True),
        lax.all_gather(ffn_gain, GROUPS, axis=0, tiled=True),
        lax.all_gather(query_gain, GROUPS, axis=0, tiled=True),
        lax.all_gather(key_gain, GROUPS, axis=0, tiled=True),
    )
    full_query, full_key, full_value, full_output, full_router = (
        gathered[0],
        gathered[1],
        gathered[2],
        gathered[3],
        gathered[4],
    )
    gain_attn = gathered[5].astype(jnp.float32)
    gain_ffn = gathered[6].astype(jnp.float32)
    gain_query = gathered[7].astype(jnp.float32)
    gain_key = gathered[8].astype(jnp.float32)
    local_heads = full_query.shape[1] // HEAD_SIZE
    seg_all = lax.all_gather(segments, CONTEXT, axis=1, tiled=True)[0]
    length = seg_all.shape[0]
    start_row = context_rank * row_count
    positions = lax.dynamic_slice_in_dim(doc_positions(seg_all), start_row, row_count)
    cosine_table, sine_table = rope_tables(positions, HEAD_SIZE)
    query_seg = segments[0]
    query_index = start_row + jnp.arange(row_count, dtype=jnp.int32)
    key_ids = jnp.arange(length, dtype=jnp.int32)
    key_block = min(512, length)

    def query_finish(raw_values, gain_vec):
        return qk_finish(raw_values, gain_vec, cosine_table[:, None, :], sine_table[:, None, :])

    def key_finish(raw_values, gain_vec):
        return qk_finish(raw_values, gain_vec, cosine_table, sine_table)

    normed_f, first_pull = jax.vjp(rms_scale, input_rows, gain_attn)
    attention_normalized = normed_f.astype(jnp.bfloat16)
    query_unrotated = matmul(attention_normalized, full_query).reshape(
        row_count, local_heads, HEAD_SIZE
    )
    key_unrotated = matmul(attention_normalized, full_key)
    value_raw = matmul(attention_normalized, full_value)
    query_f, query_pull = jax.vjp(query_finish, query_unrotated, gain_query)
    key_f, key_pull = jax.vjp(key_finish, key_unrotated, gain_key)
    query_vectors = query_f.astype(jnp.bfloat16)
    keys_all, values_all = (
        lax.all_gather(key_f.astype(jnp.bfloat16), CONTEXT, axis=0, tiled=True),
        lax.all_gather(value_raw.astype(jnp.bfloat16), CONTEXT, axis=0, tiled=True),
    )
    heads_full, log_total = attention_forward(
        query_vectors, keys_all, values_all, seg_all, query_seg, query_index, key_ids, key_block
    )
    heads_low = heads_full.reshape(row_count, local_heads * HEAD_SIZE).astype(jnp.bfloat16)
    attn_out = lax.psum(matmul_nt(heads_low, full_output).astype(jnp.bfloat16), TENSOR).astype(
        jnp.float32
    )
    residual_stream = input_rows + attn_out
    second_f, second_pull = jax.vjp(rms_scale, residual_stream, gain_ffn)
    feedforward_normalized = second_f.astype(jnp.bfloat16)
    router_scores = matmul(feedforward_normalized, full_router)
    experts_total = full_router.shape[1]
    route_ids = routes[0]
    chosen = route_ids[:, :, None] == jnp.arange(experts_total, dtype=jnp.int32)
    selected = jnp.sum(jnp.where(chosen, router_scores[:, None, :], 0.0), axis=2)
    gate_probs = jax.nn.softmax(selected, axis=-1)
    capacity = 9 * row_count * TOPK // (8 * experts_total)
    before = earlier_counts(jnp.any(chosen, axis=1)).astype(jnp.int32)
    slot_index = jnp.sum(jnp.where(chosen, before[:, None, :], 0), axis=2)
    target = jnp.where(
        slot_index < capacity, route_ids * capacity + slot_index, experts_total * capacity
    ).reshape(-1)
    source = jnp.repeat(jnp.arange(row_count, dtype=jnp.int32), TOPK)
    send_rows = (
        jnp.zeros((experts_total * capacity, model_width), jnp.bfloat16)
        .at[target]
        .set(feedforward_normalized[source], mode="drop")
    )
    expert_input_rows = to_experts(send_rows.reshape(experts_total, capacity, model_width))
    gate_activation_input = jnp.einsum(
        "phu,puo->pho", expert_input_rows, gate_weight, preferred_element_type=jnp.float32
    )
    up_activation_input = jnp.einsum(
        "phu,puo->pho", expert_input_rows, up_weight, preferred_element_type=jnp.float32
    )
    sigmoid_gate = jax.nn.sigmoid(gate_activation_input)
    silu_gate = gate_activation_input * sigmoid_gate
    hidden_middle = (silu_gate * up_activation_input).astype(jnp.bfloat16)
    expert_part = jnp.einsum(
        "pic,pcw->piw", hidden_middle, down_weight, preferred_element_type=jnp.float32
    ).astype(jnp.bfloat16)
    grad_out = cotangent[0].astype(jnp.float32)
    returned = pick_pairs(from_experts(expert_part), target, row_count)
    moe_part = jnp.sum(returned.astype(jnp.float32) * gate_probs[:, :, None], axis=1)
    moe_out = lax.psum(moe_part.astype(jnp.bfloat16), TENSOR).astype(jnp.float32)
    grad_gate_part = jnp.sum(returned.astype(jnp.float32) * grad_out[:, None, :], axis=2)
    output = (residual_stream + moe_out).astype(jnp.bfloat16)
    pair_grad = (
        (gate_probs[:, :, None] * grad_out[:, None, :])
        .astype(jnp.bfloat16)
        .reshape(row_count * TOPK, model_width)
    )
    send_grad = (
        jnp.zeros((experts_total * capacity, model_width), jnp.bfloat16)
        .at[target]
        .set(pair_grad, mode="drop")
    )
    expert_output_gradient = to_experts(send_grad.reshape(experts_total, capacity, model_width))
    grad_mid = jnp.einsum(
        "jtk,jvk->jtv", expert_output_gradient, down_weight, preferred_element_type=jnp.float32
    )
    grad_w_down = jnp.einsum(
        "tce,tci->tei", hidden_middle, expert_output_gradient, preferred_element_type=jnp.float32
    )
    gate_activation_gradient = (
        grad_mid
        * up_activation_input
        * sigmoid_gate
        * (1.0 + gate_activation_input * (1.0 - sigmoid_gate))
    ).astype(jnp.bfloat16)
    up_activation_gradient = (grad_mid * silu_gate).astype(jnp.bfloat16)
    grad_w_gate = jnp.einsum(
        "ahw,ahp->awp",
        expert_input_rows,
        gate_activation_gradient,
        preferred_element_type=jnp.float32,
    )
    grad_w_up = jnp.einsum(
        "ahw,ahp->awp",
        expert_input_rows,
        up_activation_gradient,
        preferred_element_type=jnp.float32,
    )
    grad_expert_in = (
        jnp.einsum(
            "ous,ops->oup",
            gate_activation_gradient,
            gate_weight,
            preferred_element_type=jnp.float32,
        )
        + jnp.einsum(
            "ous,ops->oup", up_activation_gradient, up_weight, preferred_element_type=jnp.float32
        )
    ).astype(jnp.bfloat16)
    grad_pairs = pick_pairs(from_experts(grad_expert_in), target, row_count)
    grad_normed_part = jnp.sum(grad_pairs.astype(jnp.float32), axis=1)
    grad_normed_moe, grad_gates = (
        lax.psum(grad_normed_part.astype(jnp.bfloat16), TENSOR).astype(jnp.float32),
        lax.psum(grad_gate_part.astype(jnp.bfloat16), TENSOR).astype(jnp.float32),
    )
    grad_selected = gate_probs * (
        grad_gates - jnp.sum(gate_probs * grad_gates, axis=1, keepdims=True)
    )
    grad_logits = jnp.sum(jnp.where(chosen, grad_selected[:, :, None], 0.0), axis=1).astype(
        jnp.bfloat16
    )
    grad_router = matmul_tn(feedforward_normalized, grad_logits)
    grad_normed_two = grad_normed_moe + matmul_nt(grad_logits, full_router)
    grad_resid_norm, grad_gain_ffn = second_pull(grad_normed_two)
    grad_resid = grad_out + grad_resid_norm
    grad_attn = grad_resid.astype(jnp.bfloat16)
    grad_w_output = matmul_tn(grad_attn, heads_low)
    grad_heads = (
        matmul(grad_attn, full_output)
        .astype(jnp.bfloat16)
        .reshape(row_count, local_heads, HEAD_SIZE)
    )
    row_delta = jnp.sum(grad_heads.astype(jnp.float32) * heads_full, axis=2).T
    grad_query, grad_key_terms, grad_value_terms = attention_backward(
        query_vectors,
        keys_all,
        values_all,
        seg_all,
        query_seg,
        query_index,
        key_ids,
        key_block,
        log_total,
        grad_heads,
        row_delta,
    )
    grad_key_local, grad_value_local = (
        lax.psum_scatter(
            grad_key_terms.astype(jnp.bfloat16), CONTEXT, scatter_dimension=0, tiled=True
        ).astype(jnp.float32),
        lax.psum_scatter(
            grad_value_terms.astype(jnp.bfloat16), CONTEXT, scatter_dimension=0, tiled=True
        ).astype(jnp.float32),
    )
    grad_query_raw, grad_gain_query = query_pull(grad_query)
    grad_key_raw, grad_gain_key = key_pull(grad_key_local)
    grad_query_low = grad_query_raw.reshape(row_count, local_heads * HEAD_SIZE).astype(jnp.bfloat16)
    grad_key_low = grad_key_raw.astype(jnp.bfloat16)
    grad_value_low = grad_value_local.astype(jnp.bfloat16)
    grad_w_query = matmul_tn(attention_normalized, grad_query_low)
    grad_w_key = matmul_tn(attention_normalized, grad_key_low)
    grad_w_value = matmul_tn(attention_normalized, grad_value_low)
    grad_normed_one = (
        matmul_nt(grad_query_low, full_query)
        + matmul_nt(grad_key_low, full_key)
        + matmul_nt(grad_value_low, full_value)
    )
    grad_normed_one, grad_gain_query, grad_gain_key = (
        lax.psum(grad_normed_one.astype(jnp.bfloat16), TENSOR).astype(jnp.float32),
        lax.psum(grad_gain_query.astype(jnp.bfloat16), TENSOR).astype(jnp.float32),
        lax.psum(grad_gain_key.astype(jnp.bfloat16), TENSOR).astype(jnp.float32),
    )
    grad_inputs_norm, grad_gain_attn = first_pull(grad_normed_one)
    input_grad = grad_resid + grad_inputs_norm
    owned = (
        lax.psum_scatter(
            grad_w_query.astype(jnp.bfloat16), GROUPS, scatter_dimension=0, tiled=True
        ).astype(jnp.float32),
        lax.psum_scatter(
            grad_w_key.astype(jnp.bfloat16), GROUPS, scatter_dimension=0, tiled=True
        ).astype(jnp.float32),
        lax.psum_scatter(
            grad_w_value.astype(jnp.bfloat16), GROUPS, scatter_dimension=0, tiled=True
        ).astype(jnp.float32),
        lax.psum_scatter(
            grad_w_output.astype(jnp.bfloat16), GROUPS, scatter_dimension=0, tiled=True
        ).astype(jnp.float32),
        lax.psum_scatter(
            grad_router.astype(jnp.bfloat16), GROUPS, scatter_dimension=0, tiled=True
        ).astype(jnp.float32),
        lax.psum_scatter(
            grad_gain_attn.astype(jnp.bfloat16),
            GROUPS,
            scatter_dimension=0,
            tiled=True,
        ).astype(jnp.float32),
        lax.psum_scatter(
            grad_gain_ffn.astype(jnp.bfloat16), GROUPS, scatter_dimension=0, tiled=True
        ).astype(jnp.float32),
        lax.psum_scatter(
            grad_gain_query.astype(jnp.bfloat16),
            GROUPS,
            scatter_dimension=0,
            tiled=True,
        ).astype(jnp.float32),
        lax.psum_scatter(
            grad_gain_key.astype(jnp.bfloat16), GROUPS, scatter_dimension=0, tiled=True
        ).astype(jnp.float32),
    )
    return (
        output[None],
        input_grad[None],
        owned[5],
        owned[0],
        owned[1],
        owned[2],
        owned[3],
        owned[7],
        owned[8],
        owned[6],
        owned[4],
        grad_w_gate,
        grad_w_up,
        grad_w_down,
    )


MESH = pl.DeviceIdType.MESH
Z_UP, Z_DOWN, Y_SIDE, X_SIDE, CORE_SIDE = range(5)

def coords():
    z, y, t = lax.axis_index(FSDP), lax.axis_index(CONTEXT), lax.axis_index(TENSOR)
    return z, y, t // 2, t % 2

def partner(z, index):
    return (z, z + 1 - 2 * (z % 2), 2 - z // 2, 3 - 3 * (z // 2))[index]

def greet(neighbours):
    barrier = pltpu.get_barrier_semaphore()
    for condition, device in neighbours:
        def tell(device=device):
            pl.semaphore_signal(barrier, inc=1, device_id=device, device_id_type=MESH)
        if condition is None: tell()
        else: pl.when(condition)(tell)
    count = sum(1 if condition is None else condition.astype(jnp.int32) for condition, device in neighbours)
    pl.semaphore_wait(barrier, count)


def spread(x_ref, out_ref, own_sem, send_sems, recv_sems):
    rows = x_ref.shape[0]; half = rows // 2
    z, y, x, c = coords()
    side = {Z_UP: (z + 1, y, 2 * x + c), Z_DOWN: (z - 1, y, 2 * x + c), Y_SIDE: (z, 1 - y, 2 * x + c),
            X_SIDE: (z, y, 2 * (1 - x) + c), CORE_SIDE: (z, y, 2 * x + 1 - c)}
    def device(zz, yy, xx, cc): return (zz * 2 + yy) * 4 + xx * 2 + cc
    def place(owner, h): return out_ref.at[pl.ds(pl.multiple_of(owner * rows + h * half, half), half)]
    def copy(link, owner, h, own=False):
        src = x_ref.at[pl.ds(h * half, half)] if own else place(owner, h)
        return pltpu.make_async_remote_copy(src_ref=src, dst_ref=place(owner, h), send_sem=send_sems.at[link, owner, h],
            recv_sem=recv_sems.at[owner, h], device_id=side[link], device_id_type=MESH)
    sent = []
    def start(link, owner, h, own=False, condition=None):
        one = copy(link, owner, h, own)
        sent.append((one, condition))
        if condition is None: one.start()
        else: pl.when(condition)(one.start)
    def arrived(owner, h): copy(CORE_SIDE, owner, h).wait_recv()
    me = device(z, y, x, c)
    keep = pltpu.make_async_copy(x_ref, out_ref.at[pl.ds(pl.multiple_of(me * rows, rows), rows)], own_sem)
    keep.start()
    def stage1(i):
        zz = partner(z, i); owner = device(zz, y, x, c); own = i == 0
        if not own:
            arrived(owner, 0); arrived(owner, 1)
        for h in range(2):
            start(Z_UP, owner, h, own, (z < 3) if own else (z < 3) & (zz < z))
            start(Z_DOWN, owner, h, own, (z > 0) if own else (z > 0) & (zz > z))
        start(Y_SIDE, owner, 0, own); start(X_SIDE, owner, 1, own)
        start(Y_SIDE, owner, 1, own); start(X_SIDE, owner, 0, own)
        for h in range(2): start(CORE_SIDE, owner, h, own)
    def stage2(i):
        zz = partner(z, i)
        oy, ox = device(zz, 1 - y, x, c), device(zz, y, 1 - x, c)
        arrived(oy, 0); start(X_SIDE, oy, 0); start(CORE_SIDE, oy, 0)
        arrived(ox, 1); start(Y_SIDE, ox, 1); start(CORE_SIDE, ox, 1)
        arrived(oy, 1); start(CORE_SIDE, oy, 1)
        arrived(ox, 0); start(CORE_SIDE, ox, 0)
    def stage3(i):
        o = device(partner(z, i), 1 - y, 1 - x, c)
        for h in range(2):
            arrived(o, h); start(CORE_SIDE, o, h)
    stage1(0); stage1(1); stage2(0); stage1(2); stage2(1); stage3(0); stage1(3); stage2(2); stage3(1); stage2(3); stage3(2); stage3(3)
    for i in range(4):
        for yy in range(2):
            for xx in range(2):
                for h in range(2): arrived(device(i, yy, xx, 1 - c), h)
    keep.wait()
    for one, condition in sent:
        if condition is None: one.wait_send()
        else: pl.when(condition)(one.wait_send)

def mix_kernel(heads_ref, weight_ref, input_ref, gain_ref, resid_ref, normed_ref, all_ref, part, mine, core_in, line_in, sems, recv, *gather_sems):
    z, y, x, c = coords()
    x_side, core_side = (z, y, 2 * (1 - x) + c), (z, y, 2 * x + 1 - c)
    greet([(z < 3, (z + 1, y, 2 * x + c)), (z > 0, (z - 1, y, 2 * x + c)), (None, (z, 1 - y, 2 * x + c)), (None, x_side), (None, core_side)])
    rows, width = input_ref.shape; f32, bf16 = jnp.float32, jnp.bfloat16
    def remote(src, dst, n, device):
        return pltpu.make_async_remote_copy(src_ref=src, dst_ref=dst, send_sem=sems.at[n], recv_sem=recv.at[n], device_id=device, device_id_type=MESH)
    over_core = [remote(part.at[n, 1 - c], core_in.at[n], n, core_side) for n in range(2)]
    over_x = remote(mine, line_in, 2, x_side)
    for n, xx in enumerate((1 - x, x)):
        heads = heads_ref[pl.ds(pl.multiple_of(xx * 2 * rows, 2 * rows), 2 * rows), :]
        for m in range(width // 512):
            at = pl.ds(m * 512, 512)
            value = lax.dot_general(heads, weight_ref[at, :], (((1,), (1,)), ((), ())), preferred_element_type=f32).astype(bf16)
            part[n, 0, :, at] = value[:rows]
            part[n, 1, :, at] = value[rows:]
        over_core[n].start()
    over_core[0].wait_recv()
    mine[...] = part[0, c] + core_in[0]
    over_x.start(); over_core[1].wait_recv()
    total = input_ref[...].astype(f32) + part[1, c].astype(f32) + core_in[1].astype(f32)
    over_x.wait_recv()
    total = total + line_in[...].astype(f32)
    resid_ref[...] = total
    normed_ref[...] = (total * lax.rsqrt(jnp.mean(total * total, axis=-1, keepdims=True) + EPSILON) * gain_ref[...]).astype(bf16)
    spread(normed_ref, all_ref, *gather_sems)
    for one in (*over_core, over_x): one.wait_send()

def mix_heads(heads, weight, own_input, gain, collective_id):
    rows, width = own_input.shape; D, V = pltpu.SemaphoreType.DMA, pltpu.VMEM; S = jax.ShapeDtypeStruct
    f32, bf16 = jnp.float32, jnp.bfloat16; vspec = pl.BlockSpec(memory_space=V)
    return pl.pallas_call(mix_kernel, out_shape=[S((rows, width), f32), S((rows, width), bf16), S((32 * rows, width), bf16)],
        in_specs=[vspec] * 4, out_specs=[vspec, vspec, pl.BlockSpec(memory_space=pl.ANY)],
        scratch_shapes=[V((2, 2, rows, width), bf16), V((rows, width), bf16), V((2, rows, width), bf16), V((rows, width), bf16), D((3,)), D((3,)),
            D, D((5, 32, 2)), D((32, 2))],
        compiler_params=pltpu.CompilerParams(collective_id=collective_id, has_side_effects=True, vmem_limit_bytes=32 << 20))(heads, weight, own_input, gain)

def groups_kernel(parts, count, *refs):
    ins, outs = refs[:count], refs[count:2 * count]
    keep_sems, send_sems, recv_sems = refs[2 * count:]
    z, y, x, c = coords()
    t = 2 * x + c
    side = {Z_UP: (z + 1, y, t), Z_DOWN: (z - 1, y, t), Y_SIDE: (z, 1 - y, t)}
    greet([(z < 3, side[Z_UP]), (z > 0, side[Z_DOWN]), (None, side[Y_SIDE])])
    sent = []
    def copy(link, p, owner, own=False):
        k, first, size, way = parts[p]
        dst = outs[k].at[pl.ds(pl.multiple_of(owner * ins[k].shape[0] + first, 16), size)]
        return pltpu.make_async_remote_copy(src_ref=ins[k].at[pl.ds(first, size)] if own else dst, dst_ref=dst, send_sem=send_sems.at[link, p, owner],
            recv_sem=recv_sems.at[p, owner], device_id=side[link], device_id_type=MESH)
    def start(link, p, owner, own=False, condition=None):
        one = copy(link, p, owner, own)
        sent.append((one, condition))
        if condition is None: one.start()
        else: pl.when(condition)(one.start)
    def arrived(p, owner): copy(Y_SIDE, p, owner).wait_recv()
    def along(p, owner, zz, own=False):
        start(Z_UP, p, owner, own, (z < 3) & (zz <= z)); start(Z_DOWN, p, owner, own, (z > 0) & (zz >= z))
    kept = []
    for p in range(len(parts)):
        along(p, z * 2 + y, z, True); start(Y_SIDE, p, z * 2 + y, True)
    for k in range(count):
        rows = ins[k].shape[0]
        one = pltpu.make_async_copy(ins[k], outs[k].at[pl.ds(pl.multiple_of((z * 2 + y) * rows, 16), rows)], keep_sems.at[k])
        one.start(); kept.append(one)
    def forward(p, i):
        zz = partner(z, i)
        near, far = zz * 2 + y, zz * 2 + 1 - y
        if i > 0:
            arrived(p, near); along(p, near, zz)
            if parts[p][3] == 0: start(Y_SIDE, p, near)
        if parts[p][3] == 1:
            arrived(p, far); along(p, far, zz)
    for wave in range(len(parts) + 3):
        for i in range(4):
            if 0 <= wave - i < len(parts): forward(wave - i, i)
    for p in range(len(parts)):
        if parts[p][3] == 0:
            for i in range(4): arrived(p, partner(z, i) * 2 + 1 - y)
    for one in kept: one.wait()
    for one, condition in sent:
        if condition is None: one.wait_send()
        else: pl.when(condition)(one.wait_send)

def gather_groups(arrays, parts, collective_id):
    count = len(arrays); D = pltpu.SemaphoreType.DMA
    return pl.pallas_call(functools.partial(groups_kernel, parts, count),
        out_shape=[jax.ShapeDtypeStruct((8 * a.shape[0], a.shape[1]), a.dtype) for a in arrays],
        in_specs=[pl.BlockSpec(memory_space=pl.ANY)] * count, out_specs=[pl.BlockSpec(memory_space=pl.ANY)] * count,
        scratch_shapes=[D((count,)), D((3, len(parts), 8)), D((len(parts), 8))],
        compiler_params=pltpu.CompilerParams(collective_id=collective_id, has_side_effects=True))(*arrays)

class TensorGather:
    def __init__(self, src, out, keep_sem, send_sems, recv_sems):
        self.src, self.out, self.keep_sem, self.send_sems, self.recv_sems = src, out, keep_sem, send_sems, recv_sems
        z, y, x, c = coords()
        self.x_side, self.core_side = (z, y, 2 * (1 - x) + c), (z, y, 2 * x + 1 - c)
        self.me, self.across, self.beside, self.last = 2 * x + c, 2 * (1 - x) + c, 2 * x + 1 - c, 2 * (1 - x) + 1 - c

    @staticmethod
    def scratch():
        D = pltpu.SemaphoreType.DMA
        return [D, D((3,)), D((4,))]

    def copy(self, n, owner, device, own=False):
        return pltpu.make_async_remote_copy(src_ref=self.src if own else self.out.at[owner], dst_ref=self.out.at[owner],
            send_sem=self.send_sems.at[n], recv_sem=self.recv_sems.at[owner], device_id=device, device_id_type=MESH)

    def start(self):
        self.copy(0, self.me, self.x_side, True).start()
        self.copy(1, self.me, self.core_side, True).start()
        self.keep().start()

    def keep(self): return pltpu.make_async_copy(self.src, self.out.at[self.me], self.keep_sem)

    def finish(self):
        self.copy(0, self.across, self.x_side).wait_recv()
        self.copy(2, self.across, self.core_side).start()
        self.copy(0, self.beside, self.x_side).wait_recv()
        self.copy(0, self.last, self.x_side).wait_recv()
        self.keep().wait()
        self.copy(0, self.me, self.x_side, True).wait_send()
        self.copy(1, self.me, self.core_side, True).wait_send()
        self.copy(2, self.across, self.core_side).wait_send()

def rms_pull(grad, values, inverse, gain):
    scaled = grad * gain
    return inverse * scaled - values * (inverse * inverse * inverse * jnp.mean(scaled * values, axis=-1, keepdims=True))

def pull_kernel(grad_ref, weight_ref, input_ref, gain_ref, head_gain_ref, above_ref, out_ref, part, mine, core_in, line_in, message, sems, recv, *gather):
    z, y, x, c = coords()
    x_side, core_side = (z, y, 2 * (1 - x) + c), (z, y, 2 * x + 1 - c)
    greet([(None, x_side), (None, core_side)])
    rows, width = above_ref.shape; f32, bf16 = jnp.float32, jnp.bfloat16
    def remote(src, dst, n, device):
        return pltpu.make_async_remote_copy(src_ref=src, dst_ref=dst, send_sem=sems.at[n], recv_sem=recv.at[n], device_id=device, device_id_type=MESH)
    over_core = [remote(part.at[n, 1 - c], core_in.at[n], n, core_side) for n in range(2)]
    over_x = remote(mine, line_in, 2, x_side)
    message[pl.ds(rows, 16), :] = jnp.zeros((16, width), f32).astype(bf16)
    gain_parts = [0.0] * (width // 512)
    for n, xx in enumerate((1 - x, x)):
        rows_at = pl.ds(pl.multiple_of(xx * 2 * rows, 2 * rows), 2 * rows)
        grad = grad_ref[rows_at, :]
        whole = input_ref[rows_at, :].astype(f32)
        inverse = lax.rsqrt(jnp.mean(whole * whole, axis=-1, keepdims=True) + EPSILON)
        for m in range(width // 512):
            at = pl.ds(m * 512, 512)
            value = lax.dot_general(grad, weight_ref[at, :], (((1,), (1,)), ((), ())), preferred_element_type=f32)
            part[n, 0, :, at] = value[:rows].astype(bf16)
            part[n, 1, :, at] = value[rows:].astype(bf16)
            gain_parts[m] = gain_parts[m] + jnp.sum(value * input_ref[rows_at, at].astype(f32) * inverse, axis=0, keepdims=True)
        over_core[n].start()
    first_row = lax.broadcasted_iota(jnp.int32, (16, 512), 0)
    for m in range(width // 512):
        message[pl.ds(rows, 16), pl.ds(m * 512, 512)] = jnp.where(first_row == 0, gain_parts[m], 0.0).astype(bf16)
    first_row = lax.broadcasted_iota(jnp.int32, (16, 128), 0)
    for n in range(2):
        at = (pl.ds(rows, 16), pl.ds(n * 128, 128))
        message[at] = jnp.where(first_row == 1, head_gain_ref[pl.ds(n, 1), :], message[at].astype(f32)).astype(bf16)
    over_core[0].wait_recv()
    mine[...] = part[0, c] + core_in[0]
    over_x.start(); over_core[1].wait_recv()
    own_at = pl.ds(pl.multiple_of((2 * x + c) * rows, rows), rows)
    own = input_ref[own_at, :].astype(f32)
    inverse = lax.rsqrt(jnp.mean(own * own, axis=-1, keepdims=True) + EPSILON)
    total = part[1, c].astype(f32) + core_in[1].astype(f32)
    over_x.wait_recv()
    total = total + line_in[...].astype(f32)
    message[pl.ds(0, rows), :] = (above_ref[...] + rms_pull(total, own, inverse, gain_ref[...])).astype(bf16)
    gather = TensorGather(message, out_ref, *gather)
    gather.start(); gather.finish()
    for one in (*over_core, over_x): one.wait_send()

def pull_inputs(grad, weight, inputs, gain, head_gain_grads, above, collective_id):
    rows, width = above.shape; D, V = pltpu.SemaphoreType.DMA, pltpu.VMEM
    bf16 = jnp.bfloat16; vspec = pl.BlockSpec(memory_space=V)
    return pl.pallas_call(pull_kernel, out_shape=jax.ShapeDtypeStruct((4, rows + 16, width), bf16),
        in_specs=[vspec] * 6, out_specs=pl.BlockSpec(memory_space=pl.ANY),
        scratch_shapes=[V((2, 2, rows, width), bf16), V((rows, width), bf16), V((2, rows, width), bf16), V((rows, width), bf16), V((rows + 16, width), bf16),
            D((3,)), D((3,)), *TensorGather.scratch()],
        compiler_params=pltpu.CompilerParams(collective_id=collective_id, has_side_effects=True, vmem_limit_bytes=40 << 20))(
            grad, weight, inputs, gain, head_gain_grads, above)


def nt(a, b):
    return lax.dot_general(a, b, (((1,), (1,)), ((), ())), preferred_element_type=jnp.float32)

def nn(a, b):
    return jnp.dot(a, b, preferred_element_type=jnp.float32)

def nearest(z, index):
    choice = [partner(z, n) for n in range(4)]
    return jnp.where(index == 0, choice[0], jnp.where(index == 1, choice[1], jnp.where(index == 2, choice[2], choice[3])))

def spot(zz, yy, xx): return (zz * 2 + yy) * 2 + xx

def step_target(step):
    z, y, x, c = coords()
    n = step % 4
    return nearest(z, 3 - step // 4), jnp.where(n < 2, 1 - y, y), jnp.where(n % 2 == 0, 1 - x, x)

def step_block(ref, step):
    size = ref.shape[0] // 16
    return ref.at[pl.ds(pl.multiple_of(spot(*step_target(step)) * size, size), size)]

class Reduction:
    def __init__(self, part, mine, first_in, second_in, line_in, core_sem, first_sem, second_sem, line_send, line_recv):
        self.part, self.mine, self.first_in, self.second_in, self.line_in = part, mine, first_in, second_in, line_in
        self.core_sem, self.first_sem, self.second_sem, self.line_send, self.line_recv = core_sem, first_sem, second_sem, line_send, line_recv
        self.half = part.shape[2] // 2
        z, y, x, c = self.at = coords()
        self.up, self.down = (z + 1, y, 2 * x + c), (z - 1, y, 2 * x + c)
        self.y_side, self.x_side, self.core_side = (z, 1 - y, 2 * x + c), (z, y, 2 * (1 - x) + c), (z, y, 2 * x + 1 - c)

    @staticmethod
    def scratch(rows, width, dtype):
        V, D, half = pltpu.VMEM, pltpu.SemaphoreType.DMA, rows // 2
        return [V((2, 2, rows, width), dtype), V((16, rows, width), dtype), V((2, 8, half, width), dtype),
            V((2, 4, half, width), dtype), V((2, 4, 2, half, width), dtype), D((2, 16)), D((2, 2, 8)), D((2, 2, 4)), D((4, 2)), D((2, 4, 2))]

    def greet(self):
        z = self.at[0]
        greet([(z < 3, self.up), (z > 0, self.down), (None, self.y_side), (None, self.x_side), (None, self.core_side)])

    @staticmethod
    def remote(src, dst, send, recv, device):
        return pltpu.make_async_remote_copy(src_ref=src, dst_ref=dst, send_sem=send, recv_sem=recv, device_id=device, device_id_type=MESH)

    def over_core(self, step):
        s = spot(*step_target(step))
        return self.remote(self.part.at[step % 2, 1 - self.at[3]], self.mine.at[s], self.core_sem.at[0, s], self.core_sem.at[1, s], self.core_side)

    def piece(self, zz, yy, xx, h): return self.mine.at[spot(zz, yy, xx), pl.ds(h * self.half, self.half)]

    def first(self, h, zz, other):
        z, y, x, c = self.at
        src = self.piece(zz, other, 1 - x, 0) if h == 0 else self.piece(zz, 1 - y, other, 1)
        s = zz * 2 + other
        return self.remote(src, self.first_in.at[h, s], self.first_sem.at[0, h, s], self.first_sem.at[1, h, s], self.x_side if h == 0 else self.y_side)

    def second(self, h, zz):
        z, y, x, c = self.at
        src = self.piece(zz, 1 - y, x, 0) if h == 0 else self.piece(zz, y, 1 - x, 1)
        return self.remote(src, self.second_in.at[h, zz], self.second_sem.at[0, h, zz], self.second_sem.at[1, h, zz], self.y_side if h == 0 else self.x_side)

    def line(self, h, zz, way):
        z, y, x, c = self.at
        return self.remote(self.piece(zz, y, x, h), self.line_in.at[way, zz, h], self.line_send.at[zz, h], self.line_recv.at[way, zz, h], self.up if way == 0 else self.down)

    def add(self, s, h, arrived):
        at = (s, pl.ds(h * self.half, self.half))
        self.mine[at] = self.mine[at] + arrived[...]

    def stage_core(self, step):
        zz, yy, xx = step_target(step)
        s = spot(zz, yy, xx)
        self.over_core(step).wait_recv()
        self.mine[s] += self.part[step % 2, self.at[3]]
        n = step % 4
        @pl.when(n % 2 == 0)
        def _(): self.first(0, zz, yy).start()
        @pl.when(n < 2)
        def _(): self.first(1, zz, xx).start()

    def stage_first(self, i):
        z, y, x, c = self.at
        zz = nearest(z, i)
        for n in range(2):
            for h, other in ((0, (1 - y, y)[n]), (1, (1 - x, x)[n])):
                self.first(h, zz, other).wait_recv()
                self.add(spot(zz, other, x) if h == 0 else spot(zz, y, other), h, self.first_in.at[h, zz * 2 + other])
                if n == 0: self.second(h, zz).start()

    def stage_second(self, i):
        z, y, x, c = self.at
        zz = nearest(z, i)
        for h in range(2):
            self.second(h, zz).wait_recv()
            self.add(spot(zz, y, x), h, self.second_in.at[h, zz])

    def stage_line(self, i):
        z, y, x, c = self.at
        zz = nearest(z, i)
        for h in range(2):
            for way, from_side, toward in ((0, z > 0, zz > z), (1, z < 3, zz < z)):
                @pl.when(from_side & (toward | (zz == z)))
                def _(h=h, way=way):
                    self.line(h, zz, way).wait_recv()
                    self.add(spot(zz, y, x), h, self.line_in.at[way, zz, h])
                @pl.when(toward)
                def _(h=h, way=way): self.line(h, zz, way).start()

    def follow(self, step):
        @pl.when((step >= 1) & (step <= 16))
        def _(): self.stage_core(step - 1)
        q = step // 4
        @pl.when((step % 4 == 1) & (q >= 2))
        def _(): self.stage_line(5 - q)
        @pl.when((step % 4 == 1) & (q >= 1))
        def _(): self.stage_first(4 - q)
        @pl.when((step % 4 == 3) & (q >= 1))
        def _(): self.stage_second(4 - q)

    def finish(self, steps):
        z, y, x, c = self.at
        if steps == 16:
            self.stage_core(15); self.stage_line(1); self.stage_first(0); self.stage_second(0)
        self.stage_line(0)

    @property
    def own(self): return spot(*self.at[:3])

    def drain(self):
        z, y, x, c = self.at
        self.over_core(14).wait_send(); self.over_core(15).wait_send()
        for zz in range(4):
            for other in range(2):
                for h in range(2): self.first(h, zz, other).wait_send()
            for h in range(2): self.second(h, zz).wait_send()
            @pl.when(zz != z)
            def _(zz=zz):
                for h in range(2): self.line(h, zz, 0).wait_send()

def expert_kernel(normed_ref, cot_ref, code_ref, router_ref, expand_ref, place_ref, gate_ref, up_ref, down_ref,
                  resid_ref, own_normed_ref, own_chosen_ref, own_cot_ref, gain_ref,
                  grad_ref, message_ref, hid_out, gate_out, up_out, normed_in, cot_in, code_in, units, message, in_sem, units_sem, *scratch):
    reduction = Reduction(*scratch[:-3])
    gather = TensorGather(message, message_ref, *scratch[-3:])
    reduction.greet()
    part = reduction.part
    rows, width, wide = grad_ref.shape[0], normed_ref.shape[1], gate_ref.shape[1]
    f32, bf16 = jnp.float32, jnp.bfloat16
    stride = code_ref.shape[0] // 8
    def loads(step):
        slot = step % 2
        zz, yy, xx = step_target(step)
        codes = code_ref.at[pl.ds(pl.multiple_of((zz * 2 + yy) * stride, 16), rows)]
        pairs = ((step_block(normed_ref, step), normed_in), (step_block(cot_ref, step), cot_in), (codes, code_in))
        return [pltpu.make_async_copy(src, dst.at[slot], in_sem.at[n, slot]) for n, (src, dst) in enumerate(pairs)]
    def stores(step):
        slot = step % 2
        return [pltpu.make_async_copy(units.at[slot, n], step_block(dst, step), units_sem.at[n, slot])
                for n, dst in enumerate((hid_out, gate_out, up_out))]
    for one in loads(0): one.start()

    def compute(step):
        slot = step % 2
        for one in loads(step): one.wait()
        @pl.when(step < 15)
        def _():
            for one in loads(step + 1): one.start()
        @pl.when(step >= 2)
        def _():
            for one in stores(step - 2): one.wait()
            reduction.over_core(step - 2).wait_send()
        normed, cot = normed_in[slot], cot_in[slot]
        code = code_in[slot].astype(f32)
        quarter = lax.broadcasted_iota(jnp.int32, code.shape, 1) // (128 // 4) - 2 * step_target(step)[2]
        code = jnp.concatenate([jnp.where(quarter == n, code, 0.0) for n in range(2)], axis=0)
        scores = jnp.where(code > 0.5, nn(normed, router_ref[...]), NEGATIVE)
        scores = jnp.where(code > 0.5, jnp.exp(scores - jnp.max(scores, axis=1, keepdims=True)), 0.0)
        gates = jnp.where(code > 1.5, scores / jnp.sum(scores, axis=1, keepdims=True), 0.0)
        high = gates.astype(bf16)
        low = (gates - high.astype(f32)).astype(bf16)
        grad_gates = jnp.zeros((2 * rows, 128), f32)
        def products(n):
            at = pl.ds(n * 256, 256)
            return (nn(normed, gate_ref[:, at]), nn(normed, up_ref[:, at]), nt(cot, down_ref[at, :]),
                nn(high, expand_ref[:, at]) + nn(low, expand_ref[:, at]))
        ahead = products(0)
        for n in range(wide // 256):
            gate_in, up_in, grad_mid, gate = ahead
            if n + 1 < wide // 256: ahead = products(n + 1)
            at = pl.ds(n * 256, 256)
            sig = lax.logistic(gate_in)
            silu = gate_in * sig
            hidden = silu * up_in
            grad_gates += nn(jnp.where(gate != 0.0, hidden * grad_mid, 0.0).astype(bf16), place_ref[at, :])
            grad_hidden = grad_mid * gate
            units[slot, 0, :, at] = (hidden * gate).astype(bf16)
            units[slot, 1, :, at] = (grad_hidden * up_in * (sig + silu * (1.0 - sig))).astype(bf16)
            units[slot, 2, :, at] = (grad_hidden * silu).astype(bf16)
        for one in stores(step): one.start()
        gate_grad, up_grad = units[slot, 1], units[slot, 2]
        for n in range(width // 512):
            at = pl.ds(n * 512, 512)
            grad = (nt(gate_grad, gate_ref[at, :]) + nt(up_grad, up_ref[at, :])).astype(bf16)
            part[slot, 0, :, at] = grad[:rows]
            part[slot, 1, :, at] = grad[rows:]
        grad_gates = grad_gates.astype(bf16)
        part[slot, 0, :, pl.ds(width, 128)] = grad_gates[:rows]
        part[slot, 1, :, pl.ds(width, 128)] = grad_gates[rows:]
        reduction.over_core(step).start()

    @pl.loop(0, 16)
    def _(step):
        compute(step)
        reduction.follow(step)
    for step in (14, 15):
        for one in stores(step): one.wait()
    reduction.finish(16)
    every, own = pl.ds(0, width), reduction.own
    grad_gates = reduction.mine[own, :, pl.ds(width, 128)].astype(f32)
    grad_gates = grad_gates + pltpu.roll(grad_gates, 64, 1)
    grad_gates = grad_gates + pltpu.roll(grad_gates, 32, 1)
    chosen = own_chosen_ref[...].astype(f32) > 0.5
    scores = jnp.where(chosen, nn(own_normed_ref[...], router_ref[...]), NEGATIVE)
    scores = jnp.where(chosen, jnp.exp(scores - jnp.max(scores, axis=1, keepdims=True)), 0.0)
    gates = scores / jnp.sum(scores, axis=1, keepdims=True)
    grad_logits = (gates * (grad_gates - jnp.sum(gates * grad_gates, axis=1, keepdims=True))).astype(bf16)
    grad = reduction.mine[own, :, every].astype(f32) + nt(grad_logits, router_ref[...])
    values = resid_ref[...]
    inverse = lax.rsqrt(jnp.mean(values * values, axis=-1, keepdims=True) + EPSILON)
    total = own_cot_ref[...].astype(f32) + rms_pull(grad, values, inverse, gain_ref[...])
    grad_ref[...] = total
    message[pl.ds(0, rows), every] = total.astype(bf16)
    message[pl.ds(0, rows), pl.ds(width, 128)] = grad_logits
    first_row = lax.broadcasted_iota(jnp.int32, (16, width), 0)
    message[pl.ds(rows, 16), every] = jnp.where(first_row == 0, jnp.sum(grad * values * inverse, axis=0, keepdims=True), 0.0).astype(bf16)
    message[pl.ds(rows, 16), pl.ds(width, 128)] = jnp.zeros((16, 128), f32).astype(bf16)
    gather.start(); gather.finish()
    reduction.drain()

def run_experts(normed_all, cot_all, codes, router, expand, place, gate_flat, up_flat, down_flat,
                resid, own_normed, own_chosen, own_cot, gain, collective_id):
    total, width = normed_all.shape; rows = total // 32; wide = gate_flat.shape[1]
    bf16 = jnp.bfloat16; D = pltpu.SemaphoreType.DMA; V = pltpu.VMEM; W = width + 128
    anyspec, vspec = pl.BlockSpec(memory_space=pl.ANY), pl.BlockSpec(memory_space=V)
    unit = jax.ShapeDtypeStruct((total, wide), bf16)
    return pl.pallas_call(expert_kernel,
        out_shape=[jax.ShapeDtypeStruct((rows, width), jnp.float32), jax.ShapeDtypeStruct((4, rows + 16, W), bf16), unit, unit, unit],
        in_specs=[anyspec] * 3 + [vspec] * 11, out_specs=[vspec] + [anyspec] * 4,
        scratch_shapes=[V((2, 2 * rows, width), bf16), V((2, 2 * rows, width), bf16), V((2, rows, 128), bf16),
            V((2, 3, 2 * rows, wide), bf16), V((rows + 16, W), bf16), D((3, 2)), D((3, 2)),
            *Reduction.scratch(rows, W, bf16), *TensorGather.scratch()],
        compiler_params=pltpu.CompilerParams(collective_id=collective_id, has_side_effects=True, vmem_limit_bytes=60 << 20))(
            normed_all, cot_all, codes, router, expand, place, gate_flat, up_flat, down_flat, resid, own_normed, own_chosen, own_cot, gain)

def output_kernel(normed_ref, cot_ref, hid_ref, gate_ref, up_ref, down_ref, resid_ref, out_ref, gate_out, up_out, down_out,
                  hid_in, wide_in, thin_in, own_out, hid_sem, in_sem, out_sem, *scratch):
    reduction = Reduction(*scratch[:-3])
    gather = TensorGather(own_out, out_ref, *scratch[-3:])
    reduction.greet()
    part = reduction.part
    rows, width, units = resid_ref.shape[0], normed_ref.shape[1], hid_ref.shape[1]
    f32, bf16 = jnp.float32, jnp.bfloat16
    lag = 2
    def hid_load(step): return pltpu.make_async_copy(step_block(hid_ref, step), hid_in.at[step % 2], hid_sem.at[step % 2])
    def loads(block):
        slot = block % 2
        zz, yy, xx = step_target(2 * block)
        at = pl.ds(pl.multiple_of((zz * 2 + yy) * 4 * rows, 4 * rows), 4 * rows)
        return ([pltpu.make_async_copy(src.at[at], wide_in.at[slot, n], in_sem.at[n, slot]) for n, src in enumerate((normed_ref, cot_ref))]
            + [pltpu.make_async_copy(src.at[at], thin_in.at[slot, n], in_sem.at[2 + n, slot]) for n, src in enumerate((hid_ref, gate_ref, up_ref))])
    for one in loads(0): one.start()
    hid_load(0).start()

    def inner(gate_sum, up_sum, down_sum):
        gate_sum[...] = jnp.zeros_like(gate_sum)
        up_sum[...] = jnp.zeros_like(up_sum)
        down_sum[...] = jnp.zeros_like(down_sum)

        def outputs(step):
            slot = step % 2
            hid_load(step).wait()
            @pl.when(step < 15)
            def _(): hid_load(step + 1).start()
            @pl.when(step >= 2)
            def _(): reduction.over_core(step - 2).wait_send()
            hid = hid_in[slot]
            for n in range(width // 512):
                at = pl.ds(n * 512, 512)
                value = nn(hid, down_ref[:, at]).astype(bf16)
                part[slot, 0, :, at] = value[:rows]
                part[slot, 1, :, at] = value[rows:]
            reduction.over_core(step).start()

        def down_gradient(block):
            slot = block % 2
            for one in loads(block): one.wait()
            @pl.when(block < 7)
            def _():
                for one in loads(block + 1): one.start()
            for n in range(units // 256):
                at = pl.ds(n * 256, 256)
                down_sum[at, :] += nn(thin_in[slot, 0, :, at].T, wide_in[slot, 1])

        def gate_gradients(block):
            slot = block % 2
            for n in range(width // 256):
                at = pl.ds(n * 256, 256)
                turned = wide_in[slot, 0, :, at].T
                gate_sum[at, :] += nn(turned, thin_in[slot, 1])
                up_sum[at, :] += nn(turned, thin_in[slot, 2])

        @pl.loop(0, 8 + lag)
        def _(block):
            for n, gradients in enumerate((down_gradient, gate_gradients)):
                step = 2 * block + n
                @pl.when(block < 8)
                def _(): outputs(step)
                @pl.when(block >= lag)
                def _(): gradients(block - lag)
                reduction.follow(step)
        kept = [pltpu.make_async_copy(src, dst, out_sem.at[n])
                for n, (src, dst) in enumerate(((gate_sum, gate_out), (up_sum, up_out), (down_sum, down_out)))]
        for one in kept: one.start()
        reduction.finish(16 + 2 * lag)
        own_out[...] = (resid_ref[...] + reduction.mine[reduction.own].astype(f32)).astype(bf16)
        gather.start(); gather.finish()
        reduction.drain()
        for one in kept: one.wait()
    pl.run_scoped(inner, pltpu.VMEM((width, units), f32), pltpu.VMEM((width, units), f32), pltpu.VMEM((units, width), f32))

def run_outputs(normed_all, cot_all, hidden_gated, gate_grad, up_grad, down_flat, resid, collective_id):
    total, width = normed_all.shape; rows = total // 32; units = hidden_gated.shape[1]
    f32, bf16 = jnp.float32, jnp.bfloat16; D = pltpu.SemaphoreType.DMA; V = pltpu.VMEM; S = jax.ShapeDtypeStruct
    anyspec, vspec = pl.BlockSpec(memory_space=pl.ANY), pl.BlockSpec(memory_space=V)
    return pl.pallas_call(output_kernel,
        out_shape=[S((4, rows, width), bf16), S((width, units), f32), S((width, units), f32), S((units, width), f32)],
        in_specs=[anyspec] * 5 + [vspec] * 2, out_specs=[anyspec] * 4,
        scratch_shapes=[V((2, 2 * rows, units), bf16), V((2, 2, 4 * rows, width), bf16), V((2, 3, 4 * rows, units), bf16), V((rows, width), bf16), D((2,)), D((5, 2)), D((3,)),
            *Reduction.scratch(rows, width, bf16), *TensorGather.scratch()],
        compiler_params=pltpu.CompilerParams(collective_id=collective_id, has_side_effects=True, vmem_limit_bytes=62 << 20))(
            normed_all, cot_all, hidden_gated, gate_grad, up_grad, down_flat, resid)


def inverse_rms(values):
    return lax.rsqrt(jnp.mean(values * values, axis=-1, keepdims=True) + EPSILON)

def attend_kernel(x_ref, gain_ref, qkv_ref, cos_ref, sin_ref, head_gain_ref, seg_rows_ref, seg_cols_ref,
                  normed_ref, raw_ref, q_ref, kv_ref, kv_other_ref, full_ref, heads_ref, lse_ref, bias, send_sem, recv_sem):
    z, y, x, c = coords()
    other = (z, 1 - y, 2 * x + c)
    greet([(None, other)])
    f32, bf16 = jnp.float32, jnp.bfloat16
    rows = x_ref.shape[0]; heads = q_ref.shape[1] // HEAD_SIZE; q_width = heads * HEAD_SIZE
    values = x_ref[...].astype(f32)
    normed_ref[...] = (values * inverse_rms(values) * gain_ref[...]).astype(bf16)
    def finish(raw, n):
        normed = raw * inverse_rms(raw) * head_gain_ref[pl.ds(n, 1), :]
        return (normed * cos_ref[...] + pltpu.roll(normed, HEAD_SIZE // 2, 1) * sin_ref[...]).astype(bf16)
    raw_kv = nn(normed_ref[...], qkv_ref[:, pl.ds(q_width, 2 * HEAD_SIZE)])
    raw_ref[:, pl.ds(q_width, HEAD_SIZE)] = raw_kv[:, :HEAD_SIZE]
    kv_ref[:, pl.ds(0, HEAD_SIZE)] = finish(raw_kv[:, :HEAD_SIZE], 1)
    kv_ref[:, pl.ds(HEAD_SIZE, HEAD_SIZE)] = raw_kv[:, HEAD_SIZE:].astype(bf16)
    move = pltpu.make_async_remote_copy(src_ref=kv_ref, dst_ref=kv_other_ref, send_sem=send_sem, recv_sem=recv_sem,
        device_id=other, device_id_type=MESH)
    @pl.when(y == 0)
    def _():
        move.start()
        kv_other_ref[...] = jnp.zeros_like(kv_other_ref)
    @pl.loop(0, heads // 2)
    def _(n):
        at = pl.ds(pl.multiple_of(n * 2 * HEAD_SIZE, 2 * HEAD_SIZE), 2 * HEAD_SIZE)
        raw = nn(normed_ref[...], qkv_ref[:, at])
        raw_ref[:, at] = raw
        for m in range(2):
            one = pl.ds(pl.multiple_of((2 * n + m) * HEAD_SIZE, HEAD_SIZE), HEAD_SIZE)
            q_ref[:, one] = finish(raw[:, m * HEAD_SIZE:(m + 1) * HEAD_SIZE], 0)
    row_id = lax.broadcasted_iota(jnp.int32, (rows, rows), 0)
    col_id = lax.broadcasted_iota(jnp.int32, (rows, rows), 1)
    bias[0] = jnp.where((seg_rows_ref[...] == seg_cols_ref[pl.ds(0, 1), :]) & (col_id <= row_id), 0.0, NEGATIVE)
    bias[1] = jnp.where(seg_rows_ref[...] == seg_cols_ref[pl.ds(1, 1), :], 0.0, NEGATIVE)
    lse_ref[...] = jnp.zeros_like(lse_ref)
    scale = HEAD_SIZE ** -0.5
    lane = lax.broadcasted_iota(jnp.int32, (rows, HEAD_SIZE), 1)
    def head(h, blocks):
        at = pl.ds(pl.multiple_of(h * HEAD_SIZE, HEAD_SIZE), HEAD_SIZE)
        query = q_ref[:, at]
        refs = (kv_ref, kv_other_ref)[:blocks]
        scores = [nt(query, ref[:, pl.ds(0, HEAD_SIZE)]) * scale + bias[n] for n, ref in enumerate(refs)]
        top = functools.reduce(jnp.maximum, [jnp.max(s, axis=1, keepdims=True) for s in scores])
        weights = [jnp.exp(s - top) for s in scores]
        total = sum(jnp.sum(w, axis=1, keepdims=True) for w in weights)
        inverse = 1.0 / total
        full = sum(nn((w * inverse).astype(bf16), ref[:, pl.ds(HEAD_SIZE, HEAD_SIZE)]) for w, ref in zip(weights, refs))
        full_ref[:, at] = full
        heads_ref[:, at] = full.astype(bf16)
        lse_ref[...] = jnp.where(lane == h, top + jnp.log(total), lse_ref[...])
    @pl.when(y == 0)
    def _():
        @pl.loop(0, heads)
        def _(h): head(h, 1)
        move.wait_send()
    @pl.when(y == 1)
    def _():
        move.wait_recv()
        @pl.loop(0, heads)
        def _(h): head(h, 2)

def attend(x, gain, qkv, cos, sin, head_gains, seg_rows, seg_cols, collective_id):
    rows, width = x.shape; q_width = qkv.shape[1] - 2 * HEAD_SIZE
    V = pltpu.VMEM; f32, bf16 = jnp.float32, jnp.bfloat16; S = jax.ShapeDtypeStruct
    vspec = pl.BlockSpec(memory_space=V)
    return pl.pallas_call(attend_kernel,
        out_shape=[S((rows, width), bf16), S((rows, q_width + HEAD_SIZE), f32), S((rows, q_width), bf16), S((rows, 2 * HEAD_SIZE), bf16),
            S((rows, 2 * HEAD_SIZE), bf16), S((rows, q_width), f32), S((rows, q_width), bf16), S((rows, HEAD_SIZE), f32)],
        in_specs=[vspec] * 8, out_specs=[vspec] * 8,
        scratch_shapes=[V((2, rows, rows), f32), pltpu.SemaphoreType.DMA, pltpu.SemaphoreType.DMA],
        compiler_params=pltpu.CompilerParams(collective_id=collective_id, has_side_effects=True, vmem_limit_bytes=48 << 20))(
            x, gain, qkv, cos, sin, head_gains, seg_rows, seg_cols)

def attend_back_kernel(cot_ref, out_w_ref, q_ref, kv_ref, kv_other_ref, raw_ref, full_ref, lse_ref, cos_ref, sin_ref, head_gain_ref,
                       seg_rows_ref, seg_cols_ref, grad_ref, gains_ref, grad_heads, delta, stats, bias, grad_q, grad_kv, kv_send, kv_in, send_sem, recv_sem):
    z, y, x, c = coords()
    other = (z, 1 - y, 2 * x + c)
    greet([(None, other)])
    f32, bf16 = jnp.float32, jnp.bfloat16
    rows = q_ref.shape[0]; heads = q_ref.shape[1] // HEAD_SIZE; q_width = heads * HEAD_SIZE
    scale = HEAD_SIZE ** -0.5
    lane = lax.broadcasted_iota(jnp.int32, (rows, HEAD_SIZE), 1)
    delta[...] = jnp.zeros_like(delta)
    @pl.loop(0, heads // 2)
    def _(n):
        at = pl.ds(pl.multiple_of(n * 2 * HEAD_SIZE, 2 * HEAD_SIZE), 2 * HEAD_SIZE)
        grad = nn(cot_ref[...], out_w_ref[:, at]).astype(bf16)
        grad_heads[:, at] = grad
        product = grad.astype(f32) * full_ref[:, at]
        for m in range(2):
            one = jnp.sum(product[:, m * HEAD_SIZE:(m + 1) * HEAD_SIZE], axis=1, keepdims=True)
            delta[...] = jnp.where(lane == 2 * n + m, one, delta[...])
    stats[0] = lse_ref[...].T
    stats[1] = delta[...].T
    key_id = lax.broadcasted_iota(jnp.int32, (rows, rows), 0)
    query_id = lax.broadcasted_iota(jnp.int32, (rows, rows), 1)
    def block(ref, seg_keys, causal):
        same = seg_keys == seg_cols_ref[pl.ds(0, 1), :]
        bias[...] = jnp.where(same & (key_id <= query_id) if causal else same, 0.0, NEGATIVE)
        grad_kv[...] = jnp.zeros_like(grad_kv)
        key, value = ref[:, pl.ds(0, HEAD_SIZE)], ref[:, pl.ds(HEAD_SIZE, HEAD_SIZE)]
        @pl.loop(0, heads)
        def _(h):
            at = pl.ds(pl.multiple_of(h * HEAD_SIZE, HEAD_SIZE), HEAD_SIZE)
            query, grad = q_ref[:, at], grad_heads[:, at]
            probs = jnp.exp(nt(key, query) * scale + bias[...] - stats[0, pl.ds(h, 1), :])
            grad_scores = (probs * (nt(value, grad) - stats[1, pl.ds(h, 1), :])).astype(bf16)
            grad_kv[:, pl.ds(0, HEAD_SIZE)] += nn(grad_scores, query) * scale
            grad_kv[:, pl.ds(HEAD_SIZE, HEAD_SIZE)] += nn(probs.astype(bf16), grad)
            grad_q[:, at] += lax.dot_general(grad_scores, key, (((0,), (0,)), ((), ())), preferred_element_type=f32) * scale
    grad_q[...] = jnp.zeros_like(grad_q)
    move = pltpu.make_async_remote_copy(src_ref=kv_send, dst_ref=kv_in, send_sem=send_sem, recv_sem=recv_sem, device_id=other, device_id_type=MESH)
    @pl.when(y == 1)
    def _():
        block(kv_other_ref, seg_rows_ref[1], False)
        kv_send[...] = grad_kv[...].astype(bf16)
        move.start()
    block(kv_ref, seg_rows_ref[0], True)
    @pl.when(y == 0)
    def _():
        move.wait_recv()
        grad_kv[...] += kv_in[...].astype(f32)
    def pull(grad, raw, n):
        turned = grad * cos_ref[...] - pltpu.roll(grad, HEAD_SIZE // 2, 1) * sin_ref[...]
        inverse = inverse_rms(raw)
        unit = raw * inverse
        gains_ref[pl.ds(n, 1), :] += jnp.sum(turned * unit, axis=0, keepdims=True)
        scaled = turned * head_gain_ref[pl.ds(n, 1), :]
        return (inverse * (scaled - unit * jnp.mean(scaled * unit, axis=1, keepdims=True))).astype(bf16)
    gains_ref[...] = jnp.zeros_like(gains_ref)
    @pl.loop(0, heads)
    def _(h):
        at = pl.ds(pl.multiple_of(h * HEAD_SIZE, HEAD_SIZE), HEAD_SIZE)
        grad_ref[:, at] = pull(grad_q[:, at], raw_ref[:, at], 0)
    at = pl.ds(q_width, HEAD_SIZE)
    grad_ref[:, at] = pull(grad_kv[:, pl.ds(0, HEAD_SIZE)], raw_ref[:, at], 1)
    grad_ref[:, pl.ds(q_width + HEAD_SIZE, HEAD_SIZE)] = grad_kv[:, pl.ds(HEAD_SIZE, HEAD_SIZE)].astype(bf16)
    @pl.when(y == 1)
    def _(): move.wait_send()

def attend_back(cot, out_w, q, kv, kv_other, raw, full, lse, cos, sin, head_gains, seg_rows, seg_cols, collective_id):
    rows, q_width = q.shape
    V = pltpu.VMEM; f32, bf16 = jnp.float32, jnp.bfloat16; S = jax.ShapeDtypeStruct
    vspec = pl.BlockSpec(memory_space=V)
    return pl.pallas_call(attend_back_kernel,
        out_shape=[S((rows, q_width + 2 * HEAD_SIZE), bf16), S((8, HEAD_SIZE), f32)],
        in_specs=[vspec] * 13, out_specs=[vspec] * 2,
        scratch_shapes=[V((rows, q_width), bf16), V((rows, HEAD_SIZE), f32), V((2, HEAD_SIZE, rows), f32), V((rows, rows), f32), V((rows, q_width), f32),
            V((rows, 2 * HEAD_SIZE), f32), V((rows, 2 * HEAD_SIZE), bf16), V((rows, 2 * HEAD_SIZE), bf16), pltpu.SemaphoreType.DMA, pltpu.SemaphoreType.DMA],
        compiler_params=pltpu.CompilerParams(collective_id=collective_id, has_side_effects=True, vmem_limit_bytes=48 << 20))(
            cot, out_w, q, kv, kv_other, raw, full, lse, cos, sin, head_gains, seg_rows, seg_cols)


def gathered_local(
    hidden_in,
    attn_gain,
    w_query,
    key_weight,
    value_weight,
    w_output,
    query_gain,
    key_gain,
    ffn_gain,
    router,
    gate_weight,
    up_weight,
    down_weight,
    routes,
    segments,
    cotangent,
):
    bf16, f32 = jnp.bfloat16, jnp.float32
    context_size = lax.axis_size(CONTEXT)
    tensor_size = lax.axis_size(TENSOR)
    group_count = lax.axis_size(FSDP) * context_size
    fsdp_rank = lax.axis_index(FSDP)
    context_rank = lax.axis_index(CONTEXT)
    tensor_rank = lax.axis_index(TENSOR)
    group_rank = fsdp_rank * context_size + context_rank
    row_count, width = hidden_in.shape[1:]
    own_count = row_count // tensor_size
    own_start = tensor_rank * own_count
    local_experts, _, hidden_width = gate_weight.shape
    experts_total = router.shape[1]
    first_expert = group_rank * local_experts
    capacity = 9 * row_count * TOPK // (8 * experts_total)
    query_width = w_query.shape[1]

    expert_ids = jnp.arange(experts_total, dtype=jnp.int32)
    chosen = jnp.any(routes[0][..., None] == expert_ids, axis=1)
    kept = chosen & (earlier_counts(chosen) < capacity)
    code = chosen.astype(bf16) + kept.astype(bf16)
    chosen_own = lax.dynamic_slice_in_dim(chosen, own_start, own_count, 0)
    code = code.reshape(tensor_size, own_count, experts_total).transpose(1, 0, 2)

    pieces = (code, router, attn_gain, ffn_gain, query_gain, key_gain, segments)
    small = jnp.concatenate([piece.astype(bf16).reshape(-1) for piece in pieces])
    small = jnp.pad(small, (0, -small.size % 2048)).reshape(-1, 128)
    qkv_weight = jnp.concatenate([w_query, key_weight, value_weight], axis=1)
    pieces_of = [(0, 0, small.shape[0], 0)]
    for array in (1, 2):
        pieces_of += [(array, 0, 112, 0), (array, 112, 96, 0), (array, 208, 48, 1)]
    small, qkv_full, full_output = gather_groups((small, qkv_weight, w_output), tuple(pieces_of), 1)
    grad_out_own = lax.dynamic_slice_in_dim(cotangent[0], own_start, own_count, 0)
    grad_out_own, codes = lax.optimization_barrier((grad_out_own, small))
    grad_out_all = lax.all_gather(grad_out_own, EVERYONE, axis=0, tiled=True)
    small = small.reshape(group_count, -1)
    parts, at = [], code.size
    for piece in pieces[1:]:
        parts.append(small[:, at : at + piece.size])
        at += piece.size
    full_router = parts[0].reshape(width, experts_total)
    gain_attn, gain_ffn, gain_query, gain_key = (
        part.reshape(-1).astype(f32) for part in parts[1:5]
    )
    head_gains = jnp.stack([gain_query, gain_key])
    all_segments = parts[5].astype(jnp.int32)

    own_seg = segments[0]
    first_seg = lax.dynamic_index_in_dim(all_segments, group_rank - context_rank, 0, keepdims=False)
    other_seg = lax.dynamic_index_in_dim(
        all_segments, group_rank + 1 - 2 * context_rank, 0, keepdims=False
    )
    smaller = jnp.sum((own_seg[None, :] < own_seg[:, None]).astype(jnp.int32), axis=1)
    smaller_first = jnp.sum((first_seg[None, :] < own_seg[:, None]).astype(jnp.int32), axis=1)
    positions = jnp.arange(row_count, dtype=jnp.int32) - smaller
    positions = positions + context_rank * (row_count - smaller_first)
    cosine_table, sine_table = rope_tables(positions, HEAD_SIZE)
    turn = jnp.where(jnp.arange(HEAD_SIZE) < HEAD_SIZE // 2, -1.0, 1.0)
    sine_table = sine_table * turn
    seg_rows = jnp.stack([own_seg, other_seg])

    normed_one, raw, query, kv, kv_other, heads_full, heads_low, log_total = attend(
        hidden_in[0],
        gain_attn[None],
        qkv_full,
        cosine_table,
        sine_table,
        head_gains,
        own_seg[:, None],
        seg_rows,
        8,
    )
    input_own = lax.dynamic_slice_in_dim(hidden_in[0], own_start, own_count, 0)
    residual_own, normed_own, normed_all = mix_heads(
        heads_low, full_output, input_own, gain_ffn[None], 3
    )

    units = local_experts * hidden_width
    gate_flat = gate_weight.transpose(1, 0, 2).reshape(width, units)
    up_flat = up_weight.transpose(1, 0, 2).reshape(width, units)
    down_flat = down_weight.reshape(units, width)
    unit_expert = first_expert + jnp.arange(units, dtype=jnp.int32) // hidden_width
    lane_ids = jnp.arange(tensor_size * experts_total, dtype=jnp.int32)
    expand = (lane_ids[:, None] % experts_total == unit_expert[None, :]).astype(bf16)
    column = tensor_rank * experts_total + unit_expert
    place = (column[:, None] == lane_ids[None, :]).astype(bf16)
    router_lanes = jnp.concatenate([full_router] * tensor_size, axis=1)
    grad_resid_own, message, hidden_gated, gate_grad, up_grad = run_experts(
        normed_all,
        grad_out_all,
        codes,
        router_lanes,
        expand,
        place,
        gate_flat,
        up_flat,
        down_flat,
        residual_own,
        normed_own,
        jnp.pad(chosen_own.astype(bf16), ((0, 0), (0, 128 - experts_total))),
        grad_out_own,
        gain_ffn[None],
        4,
    )
    grad_attn = message[:, :own_count, :width].reshape(row_count, width)
    grad_raw, head_gain_grads = attend_back(
        grad_attn,
        full_output,
        query,
        kv,
        kv_other,
        raw,
        heads_full,
        log_total,
        cosine_table,
        sine_table,
        head_gains,
        seg_rows[:, :, None],
        seg_rows,
        9,
    )
    group_logits = message[:, :own_count, width:].reshape(row_count, 128)
    grad_gain_ffn = jnp.sum(message[:, own_count, :width].astype(f32), axis=0)
    normed_group = lax.dynamic_slice_in_dim(normed_all, group_rank * row_count, row_count, 0)
    grad_router = matmul_tn(normed_group, group_logits)
    extra = jnp.where(jnp.arange(128) == experts_total, grad_gain_ffn[:, None], grad_router)
    grad_w_output = jnp.concatenate([matmul_tn(grad_attn, heads_low), extra], axis=1)
    grad_w_output = lax.psum_scatter(
        grad_w_output.astype(bf16), GROUPS, scatter_dimension=0, tiled=True
    )

    message = pull_inputs(
        grad_raw, qkv_full, hidden_in[0], gain_attn[None], head_gain_grads, grad_resid_own, 6
    )
    input_grad = message[:, :own_count].reshape(row_count, width).astype(f32)
    gain_rows = jnp.sum(message[:, own_count : own_count + 2].astype(f32), axis=0)
    head_gains_grad = jnp.pad(
        gain_rows[1, : 2 * HEAD_SIZE].reshape(2, group_count, -1),
        ((0, 0), (0, 0), (0, (width - HEAD_SIZE) // group_count)),
    ).reshape(2, width)
    extra = jnp.pad(
        jnp.stack([gain_rows[0], head_gains_grad[0], head_gains_grad[1]], axis=1),
        ((0, 0), (0, 125)),
    )
    grad_qkv = jnp.concatenate([matmul_tn(normed_one, grad_raw), extra], axis=1)
    grad_qkv, hidden_gated = lax.optimization_barrier((grad_qkv.astype(bf16), hidden_gated))
    grad_qkv = lax.psum_scatter(grad_qkv, GROUPS, scatter_dimension=0, tiled=True)
    output, grad_w_gate, grad_w_up, grad_w_down = run_outputs(
        normed_all, grad_out_all, hidden_gated, gate_grad, up_grad, down_flat, residual_own, 10
    )

    def by_expert(grad):
        return grad.reshape(width, local_experts, hidden_width).transpose(1, 0, 2)

    grad_w_gate, grad_w_up = by_expert(grad_w_gate), by_expert(grad_w_up)
    output = output.reshape(row_count, width)
    output, grad_w_output = lax.optimization_barrier((output, grad_w_output))
    grad_w_output = [
        grad_w_output[:, :query_width].astype(f32),
        grad_w_output[:, query_width + experts_total].astype(f32),
        grad_w_output[:, query_width : query_width + experts_total].astype(f32),
    ]
    grad_qkv, grad_w_output, grad_w_gate, grad_w_up = lax.optimization_barrier(
        (grad_qkv, grad_w_output, grad_w_gate, grad_w_up)
    )
    value_at, extra_at = query_width + HEAD_SIZE, query_width + 2 * HEAD_SIZE
    return (
        output[None],
        input_grad[None],
        grad_qkv[:, extra_at].astype(f32),
        grad_qkv[:, :query_width].astype(f32),
        grad_qkv[:, query_width:value_at].astype(f32),
        grad_qkv[:, value_at:extra_at].astype(f32),
        grad_w_output[0],
        grad_qkv[: query_gain.shape[0], extra_at + 1].astype(f32),
        grad_qkv[: key_gain.shape[0], extra_at + 2].astype(f32),
        grad_w_output[1],
        grad_w_output[2],
        grad_w_gate,
        grad_w_up,
        grad_w_down.reshape(down_weight.shape),
    )


def local(*arrays):
    sizes = tuple(lax.axis_size(name) for name in EVERYONE)
    return (gathered_local if sizes == (4, 2, 4) and arrays[9].shape[1] == 32 else routed_local)(*arrays)


def solution(mesh):
    in_specs = (
        P(FSDP, CONTEXT, None),
        P(GROUPS),
        P(GROUPS, TENSOR),
        P(GROUPS, TENSOR),
        P(GROUPS, TENSOR),
        P(GROUPS, TENSOR),
        P(GROUPS),
        P(GROUPS),
        P(GROUPS),
        P(GROUPS, None),
        P(GROUPS, None, TENSOR),
        P(GROUPS, None, TENSOR),
        P(GROUPS, TENSOR, None),
        P(FSDP, CONTEXT, None),
        P(FSDP, CONTEXT),
        P(FSDP, CONTEXT, None),
    )
    out_specs = (
        P(FSDP, CONTEXT, None),
        P(FSDP, CONTEXT, None),
        P(GROUPS),
        P(GROUPS, TENSOR),
        P(GROUPS, TENSOR),
        P(GROUPS, TENSOR),
        P(GROUPS, TENSOR),
        P(GROUPS),
        P(GROUPS),
        P(GROUPS),
        P(GROUPS, None),
        P(GROUPS, None, TENSOR),
        P(GROUPS, None, TENSOR),
        P(GROUPS, TENSOR, None),
    )
    return jax.shard_map(local, mesh=mesh, in_specs=in_specs, out_specs=out_specs, check_vma=False)
```

profile of v0, /device:TPU:0, one launch (start us, length us, event | category | flops | bytes accessed | tf_op | source)
XLA Modules:
  0.0 724.5 jit_solution(9267357762572725827)
XLA Ops:
  10.2 2.8 concatenate.23
  13.7 2.0 pad_maximum_fusion.2.refs_1_
  15.7 103.4 %shard_map.263 = (bf16[1664,128]{1,0:T(8,128)(2,1)}, bf16[2048,1280]{1,0:T(8,128)(2,1)}, bf16[2048,1024]{1,0:T(8,128)(2,1)}) custom-call(bf16[208,128]{1,0:T(8,128)(2,1)} %pad_bitcast_fusion.refs_0_, bf16[256,1280]{1,0:T(8,128)(2,1)} %pad_maximum_fusion.2.refs_1_, bf16[256,1024]{1,0:T(8,128)(2,1)} %refs_2_.1), custom_call_target="tpu_custom_call" | custom-call | tf_op jit(solution)/shard_map/pallas_call | solution.py:657
  119.0 2.1 dynamic-slice_bitcast_fusion
  124.2 4.6 copy.59.gate_ref
  128.8 4.7 copy.60.up_ref
  135.2 21.6 %shard_map.264 = (bf16[512,2048]{1,0:T(8,128)(2,1)S(1)}, f32[512,1152]{1,0:T(8,128)}, bf16[512,1024]{1,0:T(8,128)(2,1)S(1)}, bf16[512,256]{1,0:T(8,128)(2,1)S(1)...) custom-call(bf16[512,2048]{1,0:T(8,128)(2,1)} %bitcast.72, ...), custom_call_target="tpu_custom_call" | custom-call | tf_op jit(solution)/shard_map/pallas_call | solution.py:1166
  157.6 139.2 %shard_map.265 = (f32[128,2048]{1,0:T(8,128)S(1)}, bf16[128,2048]{1,0:T(8,128)(2,1)S(1)}, bf16[4096,2048]{1,0:T(8,128)(2,1)}) custom-call(bf16[512,1024]{1,0:T(8,128)(2,1)S(1)} %get-tuple-element.53.heads_ref, bf16[2048,1024]{1,0:T(8,128)(2,1)S(1)} %copy-done, bf16[128,2048]{1,0:T(8,128)(2,1)S(1)} %get-tuple-element.151.input_ref, f32[1,2048]{1,0:T(1,128)S(1)} %bitcast.77), custom_call_target="tpu_custom_call" | custom-call | tf_op jit(solution)/shard_map/pallas_call | solution.py:602
  301.5 145.8 %shard_map.266 = (f32[128,2048]{1,0:T(8,128)}, bf16[4,144,2176]{2,1,0:T(8,128)(2,1)}, bf16[4096,768]{1,0:T(8,128)(2,1)}, bf16[4096,768]{1,0:T(8,128)(2,1)}, bf16[4096,768]{1,0:T(8,128)(2,1)}) custom-call(bf16[4096,2048]{1,0:T(8,128)(2,1)} %get-tuple-element.55.normed_ref, bf16[4096,2048]{1,0:T(8,128)(2,1)} %all-gather.2.cloned.1.call-done.cot_ref, ...), custom_call_target="tpu_custom_call" | custom-call | tf_op jit(solution)/shard_map/pallas_call | solution.py:1000
  449.4 1.8 slice.83
  451.2 2.4 convolution_convert_fusion.1
  453.6 2.1 fusion
  455.7 2.5 pad_maximum_fusion.1
  460.5 31.2 %shard_map.267 = (bf16[512,1280]{1,0:T(8,128)(2,1)S(1)}, f32[8,128]{1,0:T(8,128)S(1)}) custom-call(bf16[512,2048]{1,0:T(8,128)(2,1)} %bitcast.82, bf16[2048,1024]{1,0:T(8,128)(2,1)} %get-tuple-element.54.weight_ref.out_w_ref, bf16[512,1024]{1,0:T(8,128)(2,1)S(1)} %get-tuple-element.62.q_ref, bf16[512,256]{1,0:T(8,128)(2,1)S(1)} %get-tuple-element.63.kv_ref, ...), custom_call_target="tpu_custom_call" | custom-call | tf_op jit(solution)/shard_map/pallas_call | solution.py:1245
  491.8 33.7 %shard_map.268 = bf16[4,144,2048]{2,1,0:T(8,128)(2,1)S(1)} custom-call(bf16[512,1280]{1,0:T(8,128)(2,1)S(1)} %get-tuple-element.68.grad_ref, bf16[2048,1280]{1,0:T(8,128)(2,1)S(1)} %bitcast.71, bf16[512,2048]{1,0:T(8,128)(2,1)S(1)} %bitcast.73, f32[1,2048]{1,0:T(1,128)S(1)} %bitcast.76, f32[8,128]{1,0:T(8,128)S(1)} %get-tuple-element.69.head_gain_ref, ...), custom_call_target="tpu_custom_call" | custom-call | tf_op jit(solution)/shard_map/pallas_call | solution.py:747
  525.8 5.4 convolution_convert_fusion
  531.2 3.0 pad_maximum_fusion
  534.3 129.7 %shard_map.269 = (bf16[4,128,2048]{2,1,0:T(8,128)(2,1)}, f32[2048,768]{1,0:T(8,128)}, f32[2048,768]{1,0:T(8,128)}, f32[768,2048]{1,0:T(8,128)}) custom-call(bf16[4096,2048]{1,0:T(8,128)(2,1)} %get-tuple-element.55.normed_ref, bf16[4096,2048]{1,0:T(8,128)(2,1)} %all-gather.2.cloned.1.call-done.cot_ref, bf16[4096,768]{1,0:T(8,128)(2,1)} %get-tuple-element.72.hid_ref, ...), custom_call_target="tpu_custom_call" | custom-call | tf_op jit(solution)/shard_map/pallas_call | solution.py:1089
  663.9 6.6 copy.62
  670.5 6.7 copy.63
  677.3 2.5 bitcast_convert_fusion
  683.5 15.9 %reduce-scatter.5.cloned.1.call-done = bf16[256,1408]{0,1:T(8,128)(2,1)} async-done(((bf16[2048,1408]{0,1:T(8,128)(2,1)}), bf16[256,1408]{0,1:T(8,128)(2,1)}) %reduce-scatter.5.cloned.1.call-update) | async-done | bytes 720912 | tf_op jit(solution)/shard_map/reduce_scatter | solution.py:1418
  708.1 3.2 copy.75
  711.3 6.3 copy.76
  (112 shorter events, 30.5 us)
Async XLA Ops:
  7.2 115.5 %copy-start.17 = (s32[1,512]{1,0:T(1,128)S(1)}, s32[1,512]{1,0:T(1,128)}, u32[]{:S(2)}) copy-start(s32[1,512]{1,0:T(1,128)} %param.30) | copy-start | bytes 6148
  7.2 294.3 %all-gather.2.cloned.1.call-start = ((), (), s32[]{:S(2)}) async-start(), calls=%async_computation.2 | async-start | bytes 17301504 | tf_op jit(solution)/shard_map/all_gather | solution.py:1306
  121.2 558.7 %reduce-scatter.3.cloned.1.call-start = ((), (), s32[]{:S(2)}) async-start(), calls=%async_computation.3 | async-start | bytes 5308416 | tf_op jit(solution)/shard_map/reduce_scatter | solution.py:1399
  122.9 34.7 %copy-start.13 = (f32[1,1,8,256]{3,1,2,0:T(1,128)}, f32[1,1,8,256]{3,1,2,0:T(1,128)S(1)}, u32[]{:S(2)}) copy-start(f32[1,1,8,256]{3,1,2,0:T(1,128)S(1)} %copy.70) | copy-start | bytes 24580
  135.2 22.3 %copy-start = (bf16[2048,1024]{1,0:T(8,128)(2,1)S(1)}, bf16[2048,1024]{1,0:T(8,128)(2,1)}, u32[]{:S(2)}) copy-start(bf16[2048,1024]{1,0:T(8,128)(2,1)} %get-tuple-element.54.weight_ref.out_w_ref) | copy-start | bytes 12582916
  156.8 0.7 copy-start.11
  157.5 139.3 %copy-start.6 = (bf16[512,1024]{1,0:T(8,128)(2,1)}, bf16[512,1024]{1,0:T(8,128)(2,1)S(1)}, u32[]{:S(2)}) copy-start(bf16[512,1024]{1,0:T(8,128)(2,1)S(1)} %get-tuple-element.53.heads_ref) | copy-start | bytes 3145732
  157.5 140.3 %copy-start.9 = (bf16[512,256]{1,0:T(8,128)(2,1)}, bf16[512,256]{1,0:T(8,128)(2,1)S(1)}, u32[]{:S(2)}) copy-start(bf16[512,256]{1,0:T(8,128)(2,1)S(1)} %get-tuple-element.64.kv_other_ref) | copy-start | bytes 786436
  157.5 140.3 %copy-start.14 = (bf16[512,2048]{1,0:T(8,128)(2,1)}, bf16[512,2048]{1,0:T(8,128)(2,1)S(1)}, u32[]{:S(2)}) copy-start(bf16[512,2048]{1,0:T(8,128)(2,1)S(1)} %get-tuple-element.57) | copy-start | bytes 6291460
  157.5 142.6 %copy-start.16 = (bf16[2048,32]{1,0:T(8,128)(2,1)S(1)}, bf16[2048,32]{1,0:T(8,128)(2,1)}, u32[]{:S(2)}) copy-start(bf16[2048,32]{1,0:T(8,128)(2,1)} %reshape.232) | copy-start | bytes 393220
  296.8 1.0 copy-start.3
  297.8 3.7 copy-start.8
  447.4 3.8 copy-start.7
  451.2 2.4 copy-start.15
  458.3 33.4 %slice-start = ((s8[5242880]{0:T(1024)(128)(4,1)}), s8[1048576]{0:T(1024)(128)(4,1)S(1)}, s32[]{:S(2)}) async-start(s8[5242880]{0:T(1024)(128)(4,1)} %bitcast.70), calls=%async_computation.5 | async-start | bytes 2097152
  458.3 241.2 %reduce-scatter.5.cloned.1.call-start = ((), (), s32[]{:S(2)}) async-start(), calls=%async_computation.4 | async-start | bytes 6488064 | tf_op jit(solution)/shard_map/reduce_scatter | solution.py:1418
  458.6 1.0 copy-start.10
  459.6 0.9 copy-start.12
  460.5 31.2 %slice-start.1 = ((s8[5242880]{0:T(1024)(128)(4,1)}), s8[4194304]{0:T(1024)(128)(4,1)S(1)}, s32[]{:S(2)}) async-start(s8[5242880]{0:T(1024)(128)(4,1)} %bitcast.70), calls=%async_computation.6 | async-start | bytes 8388608
  460.5 31.2 %copy-start.1 = (bf16[1,512,2048]{2,1,0:T(8,128)(2,1)S(1)}, bf16[1,512,2048]{2,1,0:T(8,128)(2,1)}, u32[]{:S(2)}) copy-start(bf16[1,512,2048]{2,1,0:T(8,128)(2,1)} %param.16) | copy-start | bytes 6291460
  460.5 31.2 %copy-start.5 = (f32[128,2048]{1,0:T(8,128)S(1)}, f32[128,2048]{1,0:T(8,128)}, u32[]{:S(2)}) copy-start(f32[128,2048]{1,0:T(8,128)} %get-tuple-element.70.above_ref) | copy-start | bytes 3145732
  491.7 33.8 %copy-start.4 = (bf16[512,1280]{1,0:T(8,128)(2,1)}, bf16[512,1280]{1,0:T(8,128)(2,1)S(1)}, u32[]{:S(2)}) copy-start(bf16[512,1280]{1,0:T(8,128)(2,1)S(1)} %get-tuple-element.68.grad_ref) | copy-start | bytes 3932164
  525.5 8.8 %copy-start.2 = (bf16[4,144,2048]{2,1,0:T(8,128)(2,1)}, bf16[4,144,2048]{2,1,0:T(8,128)(2,1)S(1)}, u32[]{:S(2)}) copy-start(bf16[4,144,2048]{2,1,0:T(8,128)(2,1)S(1)} %shard_map.268) | copy-start | bytes 7077892
  670.5 6.7 slice-start.2
Sparse Core Ops, SparseCore 0:
  121.3 146.3 all-gather.1
  458.4 93.3 reduce-scatter.2
  556.0 143.3 reduce-scatter.4
where the time goes:
time: 731 us; the launch traced here: 725 us
  Pallas kernels  605 us (83%)
  local copies, waits for them, and re-layouts  52.7 us (7%)
  other arithmetic  26.2 us (4%)
  waiting for transfers between devices  16 us (2%)
  between operations  14.7 us (2%)
  matrix products  10.2 us (1%)
    pallas_call x1, Pallas kernels, run_experts(): pl.pallas_call(expert_kernel, out_shape=[jax.ShapeDtypeStruct((rows, widt...  146 us
    pallas_call x1, Pallas kernels, mix_heads(): pl.pallas_call(mix_kernel, out_shape=[S((rows, width), f32), S((rows, wid...  139 us
    pallas_call x1, Pallas kernels, run_outputs(): pl.pallas_call(output_kernel, out_shape=[S((4, rows, width), bf16), S((wi...  130 us
    pallas_call x1, Pallas kernels, gather_groups(): pl.pallas_call(functools.partial(groups_kernel, parts, count), out_shape=...  103 us
    pallas_call x1, Pallas kernels, pull_inputs(): pl.pallas_call(pull_kernel, out_shape=jax.ShapeDtypeStruct((4, rows + 16,...  33.7 us
    pallas_call x1, Pallas kernels, attend_back(): pl.pallas_call(attend_back_kernel, out_shape=[S((rows, q_width + 2 * HEAD...  31.2 us
    pallas_call x1, Pallas kernels, attend(): pl.pallas_call(attend_kernel, out_shape=[S((rows, width), bf16), S((rows,...  21.6 us
    unnamed x53, local copies, waits for them, and re-layouts  18.2 us
  transfers between devices with their start and end apart: 3, of which 1 were waited for; matrix products, arithmetic and copies ran while one was open for 6% of the time, Pallas kernels for 49%

commit v1 on v0

--- a/solution.py
+++ b/solution.py
@@ -1051,9 +1051,11 @@
             @pl.when(block < 7)
             def _():
                 for one in loads(block + 1): one.start()
-            for n in range(units // 256):
-                at = pl.ds(n * 256, 256)
-                down_sum[at, :] += nn(thin_in[slot, 0, :, at].T, wide_in[slot, 1])
+            @pl.when(block < 7)
+            def _():
+                for n in range(units // 256):
+                    at = pl.ds(n * 256, 256)
+                    down_sum[at, :] += nn(thin_in[slot, 0, :, at].T, wide_in[slot, 1])
 
         def gate_gradients(block):
             slot = block % 2
@@ -1419,6 +1421,8 @@
     output, grad_w_gate, grad_w_up, grad_w_down = run_outputs(
         normed_all, grad_out_all, hidden_gated, gate_grad, up_grad, down_flat, residual_own, 10
     )
+    own_hidden = lax.dynamic_slice_in_dim(hidden_gated, group_rank * row_count, row_count, 0)
+    grad_w_down = grad_w_down + matmul_tn(own_hidden, cotangent[0])
 
     def by_expert(grad):
         return grad.reshape(width, local_experts, hidden_width).transpose(1, 0, 2)
@@ -1431,8 +1435,8 @@
         grad_w_output[:, query_width + experts_total].astype(f32),
         grad_w_output[:, query_width : query_width + experts_total].astype(f32),
     ]
-    grad_qkv, grad_w_output, grad_w_gate, grad_w_up = lax.optimization_barrier(
-        (grad_qkv, grad_w_output, grad_w_gate, grad_w_up)
+    grad_qkv, grad_w_output, grad_w_gate, grad_w_up, grad_w_down = lax.optimization_barrier(
+        (grad_qkv, grad_w_output, grad_w_gate, grad_w_up, grad_w_down)
     )
     value_at, extra_at = query_width + HEAD_SIZE, query_width + 2 * HEAD_SIZE
     return (

time: 731 us -> 725 us (level)
  waiting for transfers between devices: 16 us -> 3.5 us
    reduce_scatter x1, waiting for transfers between devices: 15.9 us -> 3.45 us  [gathered_local(): lax.psum_scatter(grad_qkv, GROUPS, scatter_dimension=0, tiled=True)]
    dot_general x3 -> x4, matrix products: 9.9 us -> 16.3 us  [matmul_tn(): lax.dot_general(left_side, right_side, (((0,), (0,)), ((), ())), preferre...]
    unnamed x53 -> x54, local copies, waits for them, and re-layouts: 18.2 us -> 13.6 us
  transfers between devices with their start and end apart: 3 -> 3, of which waited for: 1 -> 1; matrix products, arithmetic and copies ran while one was open for 6% -> 7% of each run, Pallas kernels for 49% -> 50%
where the time goes in v1:
time: 725 us; the launch traced here: 717 us
  Pallas kernels  608 us (84%)
  local copies, waits for them, and re-layouts  48.1 us (7%)
  other arithmetic  26.5 us (4%)
  matrix products  16.6 us (2%)
  between operations  14.5 us (2%)
    pallas_call x1, Pallas kernels, run_experts(): pl.pallas_call(expert_kernel, out_shape=[jax.ShapeDtypeStruct((rows, widt...  146 us
    pallas_call x1, Pallas kernels, mix_heads(): pl.pallas_call(mix_kernel, out_shape=[S((rows, width), f32), S((rows, wid...  138 us
    pallas_call x1, Pallas kernels, run_outputs(): pl.pallas_call(output_kernel, out_shape=[S((4, rows, width), bf16), S((wi...  133 us
    pallas_call x1, Pallas kernels, gather_groups(): pl.pallas_call(functools.partial(groups_kernel, parts, count), out_shape=...  103 us
    pallas_call x1, Pallas kernels, pull_inputs(): pl.pallas_call(pull_kernel, out_shape=jax.ShapeDtypeStruct((4, rows + 16,...  33.7 us
    pallas_call x1, Pallas kernels, attend_back(): pl.pallas_call(attend_back_kernel, out_shape=[S((rows, q_width + 2 * HEAD...  31.4 us
    pallas_call x1, Pallas kernels, attend(): pl.pallas_call(attend_kernel, out_shape=[S((rows, width), bf16), S((rows,...  21.5 us
    dot_general x4, matrix products, matmul_tn(): lax.dot_general(left_side, right_side, (((0,), (0,)), ((), ())), preferre...  16.3 us
  transfers between devices with their start and end apart: 3, of which 1 were waited for; matrix products, arithmetic and copies ran while one was open for 7% of the time, Pallas kernels for 50%

profile of v1, /device:TPU:0, one launch (start us, length us, event | category | flops | bytes accessed | tf_op | source)
XLA Modules:
  0.0 717.0 jit_solution(3200336326977922094)
XLA Ops:
  10.3 2.8 concatenate.23
  13.7 2.0 pad_maximum_fusion.2.refs_1_
  15.7 2.1 dynamic-slice_bitcast_fusion
  17.8 103.4 %shard_map.263 = (bf16[1664,128]{1,0:T(8,128)(2,1)}, bf16[2048,1280]{1,0:T(8,128)(2,1)}, bf16[2048,1024]{1,0:T(8,128)(2,1)}) custom-call(bf16[208,128]{1,0:T(8,128)(2,1)} %pad_bitcast_fusion.refs_0_, bf16[256,1280]{1,0:T(8,128)(2,1)} %pad_maximum_fusion.2.refs_1_, bf16[256,1024]{1,0:T(8,128)(2,1)} %refs_2_.1), custom_call_target="tpu_custom_call" | custom-call | tf_op jit(solution)/shard_map/pallas_call | solution.py:657
  122.7 4.6 copy.59.gate_ref
  127.4 4.7 copy.60.up_ref
  135.3 21.5 %shard_map.264 = (bf16[512,2048]{1,0:T(8,128)(2,1)S(1)}, f32[512,1152]{1,0:T(8,128)}, bf16[512,1024]{1,0:T(8,128)(2,1)S(1)}, bf16[512,256]{1,0:T(8,128)(2,1)S(1)...) custom-call(bf16[512,2048]{1,0:T(8,128)(2,1)} %bitcast.75, ...), custom_call_target="tpu_custom_call" | custom-call | tf_op jit(solution)/shard_map/pallas_call | solution.py:1168
  157.6 138.1 %shard_map.265 = (f32[128,2048]{1,0:T(8,128)S(1)}, bf16[128,2048]{1,0:T(8,128)(2,1)S(1)}, bf16[4096,2048]{1,0:T(8,128)(2,1)}) custom-call(bf16[512,1024]{1,0:T(8,128)(2,1)S(1)} %get-tuple-element.54.heads_ref, bf16[2048,1024]{1,0:T(8,128)(2,1)S(1)} %copy-done, bf16[128,2048]{1,0:T(8,128)(2,1)S(1)} %get-tuple-element.153.input_ref, f32[1,2048]{1,0:T(1,128)S(1)} %bitcast.80), custom_call_target="tpu_custom_call" | custom-call | tf_op jit(solution)/shard_map/pallas_call | solution.py:602
  300.4 146.3 %shard_map.266 = (f32[128,2048]{1,0:T(8,128)}, bf16[4,144,2176]{2,1,0:T(8,128)(2,1)}, bf16[4096,768]{1,0:T(8,128)(2,1)}, bf16[4096,768]{1,0:T(8,128)(2,1)}, bf16[4096,768]{1,0:T(8,128)(2,1)}) custom-call(bf16[4096,2048]{1,0:T(8,128)(2,1)} %get-tuple-element.56.normed_ref, bf16[4096,2048]{1,0:T(8,128)(2,1)} %all-gather.2.cloned.1.call-done.cot_ref, ...), custom_call_target="tpu_custom_call" | custom-call | tf_op jit(solution)/shard_map/pallas_call | solution.py:1000
  448.7 1.8 slice.83
  450.6 2.4 convolution_convert_fusion.1
  453.0 2.1 fusion
  455.1 2.7 pad_maximum_fusion.1
  460.0 31.4 %shard_map.267 = (bf16[512,1280]{1,0:T(8,128)(2,1)S(1)}, f32[8,128]{1,0:T(8,128)S(1)}) custom-call(bf16[512,2048]{1,0:T(8,128)(2,1)} %bitcast.86, bf16[2048,1024]{1,0:T(8,128)(2,1)} %get-tuple-element.55.weight_ref.out_w_ref, bf16[512,1024]{1,0:T(8,128)(2,1)S(1)} %get-tuple-element.63.q_ref, bf16[512,256]{1,0:T(8,128)(2,1)S(1)} %get-tuple-element.64.kv_ref, ...), custom_call_target="tpu_custom_call" | custom-call | tf_op jit(solution)/shard_map/pallas_call | solution.py:1247
  491.5 33.7 %shard_map.268 = bf16[4,144,2048]{2,1,0:T(8,128)(2,1)S(1)} custom-call(bf16[512,1280]{1,0:T(8,128)(2,1)S(1)} %get-tuple-element.69.grad_ref, bf16[2048,1280]{1,0:T(8,128)(2,1)S(1)} %bitcast.74, bf16[512,2048]{1,0:T(8,128)(2,1)S(1)} %bitcast.76, f32[1,2048]{1,0:T(1,128)S(1)} %bitcast.79, f32[8,128]{1,0:T(8,128)S(1)} %get-tuple-element.70.head_gain_ref, ...), custom_call_target="tpu_custom_call" | custom-call | tf_op jit(solution)/shard_map/pallas_call | solution.py:747
  525.5 5.4 convolution_convert_fusion
  530.9 3.0 pad_maximum_fusion
  533.9 133.2 %shard_map.269 = (bf16[4,128,2048]{2,1,0:T(8,128)(2,1)}, f32[2048,768]{1,0:T(8,128)}, f32[2048,768]{1,0:T(8,128)}, f32[768,2048]{1,0:T(8,128)}) custom-call(bf16[4096,2048]{1,0:T(8,128)(2,1)} %get-tuple-element.56.normed_ref, bf16[4096,2048]{1,0:T(8,128)(2,1)} %all-gather.2.cloned.1.call-done.cot_ref, bf16[4096,768]{1,0:T(8,128)(2,1)} %get-tuple-element.73.hid_ref, ...), custom_call_target="tpu_custom_call" | custom-call | tf_op jit(solution)/shard_map/pallas_call | solution.py:1091
  667.1 6.7 copy.62
  673.8 6.7 copy.63
  680.5 2.7 bitcast_convert_fusion
  684.8 6.4 convolution_add_fusion
  695.0 3.5 reduce-scatter.5.cloned.1.call-done
  707.0 3.2 copy.74
  (114 shorter events, 32.2 us)
Async XLA Ops:
  7.2 115.4 %copy-start.18 = (s32[1,512]{1,0:T(1,128)S(1)}, s32[1,512]{1,0:T(1,128)}, u32[]{:S(2)}) copy-start(s32[1,512]{1,0:T(1,128)} %param.30) | copy-start | bytes 6148
  7.2 293.2 %all-gather.2.cloned.1.call-start = ((), (), s32[]{:S(2)}) async-start(), calls=%async_computation.2 | async-start | bytes 17301504 | tf_op jit(solution)/shard_map/all_gather | solution.py:1308
  121.2 570.1 %reduce-scatter.3.cloned.1.call-start = ((), (), s32[]{:S(2)}) async-start(), calls=%async_computation.3 | async-start | bytes 5308416 | tf_op jit(solution)/shard_map/reduce_scatter | solution.py:1401
  132.4 25.2 %copy-start.13 = (f32[1,1,8,256]{3,1,2,0:T(1,128)}, f32[1,1,8,256]{3,1,2,0:T(1,128)S(1)}, u32[]{:S(2)}) copy-start(f32[1,1,8,256]{3,1,2,0:T(1,128)S(1)} %copy.70) | copy-start | bytes 24580
  135.3 22.3 %copy-start = (bf16[2048,1024]{1,0:T(8,128)(2,1)S(1)}, bf16[2048,1024]{1,0:T(8,128)(2,1)}, u32[]{:S(2)}) copy-start(bf16[2048,1024]{1,0:T(8,128)(2,1)} %get-tuple-element.55.weight_ref.out_w_ref) | copy-start | bytes 12582916
  157.5 138.1 %copy-start.6 = (bf16[512,1024]{1,0:T(8,128)(2,1)}, bf16[512,1024]{1,0:T(8,128)(2,1)S(1)}, u32[]{:S(2)}) copy-start(bf16[512,1024]{1,0:T(8,128)(2,1)S(1)} %get-tuple-element.54.heads_ref) | copy-start | bytes 3145732
  157.5 139.1 %copy-start.9 = (bf16[512,256]{1,0:T(8,128)(2,1)}, bf16[512,256]{1,0:T(8,128)(2,1)S(1)}, u32[]{:S(2)}) copy-start(bf16[512,256]{1,0:T(8,128)(2,1)S(1)} %get-tuple-element.65.kv_other_ref) | copy-start | bytes 786436
  157.5 139.2 %copy-start.14 = (bf16[512,2048]{1,0:T(8,128)(2,1)}, bf16[512,2048]{1,0:T(8,128)(2,1)S(1)}, u32[]{:S(2)}) copy-start(bf16[512,2048]{1,0:T(8,128)(2,1)S(1)} %get-tuple-element.58) | copy-start | bytes 6291460
  157.5 141.5 %copy-start.17 = (bf16[2048,32]{1,0:T(8,128)(2,1)S(1)}, bf16[2048,32]{1,0:T(8,128)(2,1)}, u32[]{:S(2)}) copy-start(bf16[2048,32]{1,0:T(8,128)(2,1)} %reshape.232) | copy-start | bytes 393220
  295.7 1.0 copy-start.3
  296.7 3.7 copy-start.8
  446.8 3.8 copy-start.7
  450.6 2.4 copy-start.16
  457.8 33.6 %slice-start = ((s8[5242880]{0:T(1024)(128)(4,1)}), s8[1048576]{0:T(1024)(128)(4,1)S(1)}, s32[]{:S(2)}) async-start(s8[5242880]{0:T(1024)(128)(4,1)} %bitcast.73), calls=%async_computation.5 | async-start | bytes 2097152
  457.8 240.6 %reduce-scatter.5.cloned.1.call-start = ((), (), s32[]{:S(2)}) async-start(), calls=%async_computation.4 | async-start | bytes 6488064 | tf_op jit(solution)/shard_map/reduce_scatter | solution.py:1420
  458.1 1.0 copy-start.10
  459.1 0.9 copy-start.12
  460.0 31.4 %slice-start.1 = ((s8[5242880]{0:T(1024)(128)(4,1)}), s8[4194304]{0:T(1024)(128)(4,1)S(1)}, s32[]{:S(2)}) async-start(s8[5242880]{0:T(1024)(128)(4,1)} %bitcast.73), calls=%async_computation.6 | async-start | bytes 8388608
  460.0 31.4 %copy-start.1 = (bf16[1,512,2048]{2,1,0:T(8,128)(2,1)S(1)}, bf16[1,512,2048]{2,1,0:T(8,128)(2,1)}, u32[]{:S(2)}) copy-start(bf16[1,512,2048]{2,1,0:T(8,128)(2,1)} %param.16) | copy-start | bytes 6291460
  460.0 31.4 %copy-start.5 = (f32[128,2048]{1,0:T(8,128)S(1)}, f32[128,2048]{1,0:T(8,128)}, u32[]{:S(2)}) copy-start(f32[128,2048]{1,0:T(8,128)} %get-tuple-element.71.above_ref) | copy-start | bytes 3145732
  491.4 33.8 %copy-start.4 = (bf16[512,1280]{1,0:T(8,128)(2,1)}, bf16[512,1280]{1,0:T(8,128)(2,1)S(1)}, u32[]{:S(2)}) copy-start(bf16[512,1280]{1,0:T(8,128)(2,1)S(1)} %get-tuple-element.69.grad_ref) | copy-start | bytes 3932164
  525.2 8.7 %copy-start.2 = (bf16[4,144,2048]{2,1,0:T(8,128)(2,1)}, bf16[4,144,2048]{2,1,0:T(8,128)(2,1)S(1)}, u32[]{:S(2)}) copy-start(bf16[4,144,2048]{2,1,0:T(8,128)(2,1)S(1)} %shard_map.268) | copy-start | bytes 7077892
  673.8 6.7 slice-start.2
  680.5 4.3 copy-start.15
  (1 other events, 0.7 us)
Sparse Core Ops, SparseCore 0:
  121.3 146.4 all-gather.1
  457.9 93.0 reduce-scatter.2
  554.7 143.6 reduce-scatter.4

commit v2 on v1

--- a/solution.py
+++ b/solution.py
@@ -774,17 +774,18 @@
     return ref.at[pl.ds(pl.multiple_of(spot(*step_target(step)) * size, size), size)]
 
 class Reduction:
-    def __init__(self, part, mine, first_in, second_in, line_in, core_sem, first_sem, second_sem, line_send, line_recv):
+    def __init__(self, part, mine, first_in, second_in, line_in, core_sem, first_sem, second_sem, line_send, line_recv, split):
         self.part, self.mine, self.first_in, self.second_in, self.line_in = part, mine, first_in, second_in, line_in
         self.core_sem, self.first_sem, self.second_sem, self.line_send, self.line_recv = core_sem, first_sem, second_sem, line_send, line_recv
-        self.half = part.shape[2] // 2
+        self.pieces = (pl.ds(0, split), pl.ds(split, part.shape[2] - split))
+        self.sizes = (pl.ds(0, split), pl.ds(0, part.shape[2] - split))
         z, y, x, c = self.at = coords()
         self.up, self.down = (z + 1, y, 2 * x + c), (z - 1, y, 2 * x + c)
         self.y_side, self.x_side, self.core_side = (z, 1 - y, 2 * x + c), (z, y, 2 * (1 - x) + c), (z, y, 2 * x + 1 - c)
 
     @staticmethod
-    def scratch(rows, width, dtype):
-        V, D, half = pltpu.VMEM, pltpu.SemaphoreType.DMA, rows // 2
+    def scratch(rows, width, dtype, split):
+        V, D, half = pltpu.VMEM, pltpu.SemaphoreType.DMA, max(split, rows - split)
         return [V((2, 2, rows, width), dtype), V((16, rows, width), dtype), V((2, 8, half, width), dtype),
             V((2, 4, half, width), dtype), V((2, 4, 2, half, width), dtype), D((2, 16)), D((2, 2, 8)), D((2, 2, 4)), D((4, 2)), D((2, 4, 2))]
 
@@ -800,25 +801,25 @@
         s = spot(*step_target(step))
         return self.remote(self.part.at[step % 2, 1 - self.at[3]], self.mine.at[s], self.core_sem.at[0, s], self.core_sem.at[1, s], self.core_side)
 
-    def piece(self, zz, yy, xx, h): return self.mine.at[spot(zz, yy, xx), pl.ds(h * self.half, self.half)]
+    def piece(self, zz, yy, xx, h): return self.mine.at[spot(zz, yy, xx), self.pieces[h]]
 
     def first(self, h, zz, other):
         z, y, x, c = self.at
         src = self.piece(zz, other, 1 - x, 0) if h == 0 else self.piece(zz, 1 - y, other, 1)
         s = zz * 2 + other
-        return self.remote(src, self.first_in.at[h, s], self.first_sem.at[0, h, s], self.first_sem.at[1, h, s], self.x_side if h == 0 else self.y_side)
+        return self.remote(src, self.first_in.at[h, s, self.sizes[h]], self.first_sem.at[0, h, s], self.first_sem.at[1, h, s], self.x_side if h == 0 else self.y_side)
 
     def second(self, h, zz):
         z, y, x, c = self.at
         src = self.piece(zz, 1 - y, x, 0) if h == 0 else self.piece(zz, y, 1 - x, 1)
-        return self.remote(src, self.second_in.at[h, zz], self.second_sem.at[0, h, zz], self.second_sem.at[1, h, zz], self.y_side if h == 0 else self.x_side)
+        return self.remote(src, self.second_in.at[h, zz, self.sizes[h]], self.second_sem.at[0, h, zz], self.second_sem.at[1, h, zz], self.y_side if h == 0 else self.x_side)
 
     def line(self, h, zz, way):
         z, y, x, c = self.at
-        return self.remote(self.piece(zz, y, x, h), self.line_in.at[way, zz, h], self.line_send.at[zz, h], self.line_recv.at[way, zz, h], self.up if way == 0 else self.down)
+        return self.remote(self.piece(zz, y, x, h), self.line_in.at[way, zz, h, self.sizes[h]], self.line_send.at[zz, h], self.line_recv.at[way, zz, h], self.up if way == 0 else self.down)
 
     def add(self, s, h, arrived):
-        at = (s, pl.ds(h * self.half, self.half))
+        at = (s, self.pieces[h])
         self.mine[at] = self.mine[at] + arrived[...]
 
     def stage_core(self, step):
@@ -838,7 +839,7 @@
         for n in range(2):
             for h, other in ((0, (1 - y, y)[n]), (1, (1 - x, x)[n])):
                 self.first(h, zz, other).wait_recv()
-                self.add(spot(zz, other, x) if h == 0 else spot(zz, y, other), h, self.first_in.at[h, zz * 2 + other])
+                self.add(spot(zz, other, x) if h == 0 else spot(zz, y, other), h, self.first_in.at[h, zz * 2 + other, self.sizes[h]])
                 if n == 0: self.second(h, zz).start()
 
     def stage_second(self, i):
@@ -846,7 +847,7 @@
         zz = nearest(z, i)
         for h in range(2):
             self.second(h, zz).wait_recv()
-            self.add(spot(zz, y, x), h, self.second_in.at[h, zz])
+            self.add(spot(zz, y, x), h, self.second_in.at[h, zz, self.sizes[h]])
 
     def stage_line(self, i):
         z, y, x, c = self.at
@@ -856,7 +857,7 @@
                 @pl.when(from_side & (toward | (zz == z)))
                 def _(h=h, way=way):
                     self.line(h, zz, way).wait_recv()
-                    self.add(spot(zz, y, x), h, self.line_in.at[way, zz, h])
+                    self.add(spot(zz, y, x), h, self.line_in.at[way, zz, h, self.sizes[h]])
                 @pl.when(toward)
                 def _(h=h, way=way): self.line(h, zz, way).start()
 
@@ -894,7 +895,7 @@
 def expert_kernel(normed_ref, cot_ref, code_ref, router_ref, expand_ref, place_ref, gate_ref, up_ref, down_ref,
                   resid_ref, own_normed_ref, own_chosen_ref, own_cot_ref, gain_ref,
                   grad_ref, message_ref, hid_out, gate_out, up_out, normed_in, cot_in, code_in, units, message, in_sem, units_sem, *scratch):
-    reduction = Reduction(*scratch[:-3])
+    reduction = Reduction(*scratch[:-3], split=64)
     gather = TensorGather(message, message_ref, *scratch[-3:])
     reduction.greet()
     part = reduction.part
@@ -1002,13 +1003,13 @@
         in_specs=[anyspec] * 3 + [vspec] * 11, out_specs=[vspec] + [anyspec] * 4,
         scratch_shapes=[V((2, 2 * rows, width), bf16), V((2, 2 * rows, width), bf16), V((2, rows, 128), bf16),
             V((2, 3, 2 * rows, wide), bf16), V((rows + 16, W), bf16), D((3, 2)), D((3, 2)),
-            *Reduction.scratch(rows, W, bf16), *TensorGather.scratch()],
+            *Reduction.scratch(rows, W, bf16, 64), *TensorGather.scratch()],
         compiler_params=pltpu.CompilerParams(collective_id=collective_id, has_side_effects=True, vmem_limit_bytes=60 << 20))(
             normed_all, cot_all, codes, router, expand, place, gate_flat, up_flat, down_flat, resid, own_normed, own_chosen, own_cot, gain)
 
 def output_kernel(normed_ref, cot_ref, hid_ref, gate_ref, up_ref, down_ref, resid_ref, out_ref, gate_out, up_out, down_out,
                   hid_in, wide_in, thin_in, own_out, hid_sem, in_sem, out_sem, *scratch):
-    reduction = Reduction(*scratch[:-3])
+    reduction = Reduction(*scratch[:-3], split=80)
     gather = TensorGather(own_out, out_ref, *scratch[-3:])
     reduction.greet()
     part = reduction.part
@@ -1092,7 +1093,7 @@
         out_shape=[S((4, rows, width), bf16), S((width, units), f32), S((width, units), f32), S((units, width), f32)],
         in_specs=[anyspec] * 5 + [vspec] * 2, out_specs=[anyspec] * 4,
         scratch_shapes=[V((2, 2 * rows, units), bf16), V((2, 2, 4 * rows, width), bf16), V((2, 3, 4 * rows, units), bf16), V((rows, width), bf16), D((2,)), D((5, 2)), D((3,)),
-            *Reduction.scratch(rows, width, bf16), *TensorGather.scratch()],
+            *Reduction.scratch(rows, width, bf16, 80), *TensorGather.scratch()],
         compiler_params=pltpu.CompilerParams(collective_id=collective_id, has_side_effects=True, vmem_limit_bytes=62 << 20))(
             normed_all, cot_all, hidden_gated, gate_grad, up_grad, down_flat, resid)
 
@@ -1396,8 +1397,7 @@
     grad_gain_ffn = jnp.sum(message[:, own_count, :width].astype(f32), axis=0)
     normed_group = lax.dynamic_slice_in_dim(normed_all, group_rank * row_count, row_count, 0)
     grad_router = matmul_tn(normed_group, group_logits)
-    extra = jnp.where(jnp.arange(128) == experts_total, grad_gain_ffn[:, None], grad_router)
-    grad_w_output = jnp.concatenate([matmul_tn(grad_attn, heads_low), extra], axis=1)
+    grad_w_output = matmul_tn(grad_attn, heads_low)
     grad_w_output = lax.psum_scatter(
         grad_w_output.astype(bf16), GROUPS, scatter_dimension=0, tiled=True
     )
@@ -1411,10 +1411,9 @@
         gain_rows[1, : 2 * HEAD_SIZE].reshape(2, group_count, -1),
         ((0, 0), (0, 0), (0, (width - HEAD_SIZE) // group_count)),
     ).reshape(2, width)
-    extra = jnp.pad(
-        jnp.stack([gain_rows[0], head_gains_grad[0], head_gains_grad[1]], axis=1),
-        ((0, 0), (0, 125)),
-    )
+    columns = jnp.stack([gain_rows[0], head_gains_grad[0], head_gains_grad[1], grad_gain_ffn], axis=1)
+    extra = jnp.concatenate([columns, grad_router[:, :experts_total]], axis=1)
+    extra = jnp.pad(extra, ((0, 0), (0, 128 - extra.shape[1])))
     grad_qkv = jnp.concatenate([matmul_tn(normed_one, grad_raw), extra], axis=1)
     grad_qkv, hidden_gated = lax.optimization_barrier((grad_qkv.astype(bf16), hidden_gated))
     grad_qkv = lax.psum_scatter(grad_qkv, GROUPS, scatter_dimension=0, tiled=True)
@@ -1430,11 +1429,7 @@
     grad_w_gate, grad_w_up = by_expert(grad_w_gate), by_expert(grad_w_up)
     output = output.reshape(row_count, width)
     output, grad_w_output = lax.optimization_barrier((output, grad_w_output))
-    grad_w_output = [
-        grad_w_output[:, :query_width].astype(f32),
-        grad_w_output[:, query_width + experts_total].astype(f32),
-        grad_w_output[:, query_width : query_width + experts_total].astype(f32),
-    ]
+    grad_w_output = grad_w_output.astype(f32)
     grad_qkv, grad_w_output, grad_w_gate, grad_w_up, grad_w_down = lax.optimization_barrier(
         (grad_qkv, grad_w_output, grad_w_gate, grad_w_up, grad_w_down)
     )
@@ -1446,11 +1441,11 @@
         grad_qkv[:, :query_width].astype(f32),
         grad_qkv[:, query_width:value_at].astype(f32),
         grad_qkv[:, value_at:extra_at].astype(f32),
-        grad_w_output[0],
+        grad_w_output,
         grad_qkv[: query_gain.shape[0], extra_at + 1].astype(f32),
         grad_qkv[: key_gain.shape[0], extra_at + 2].astype(f32),
-        grad_w_output[1],
-        grad_w_output[2],
+        grad_qkv[:, extra_at + 3].astype(f32),
+        grad_qkv[:, extra_at + 4 : extra_at + 4 + experts_total].astype(f32),
         grad_w_gate,
         grad_w_up,
         grad_w_down.reshape(down_weight.shape),

time: 725 us -> 752 us (1.037)
  Pallas kernels: 608 us -> 632 us
    pallas_call x1, Pallas kernels: 133 us -> 153 us  [run_outputs(): pl.pallas_call(output_kernel, out_shape=[S((4, rows, width), bf16), S((wi...]
  transfers between devices with their start and end apart: 3 -> 3, of which waited for: 1 -> 0; matrix products, arithmetic and copies ran while one was open for 7% -> 8% of each run, Pallas kernels for 50% -> 52%
where the time goes in v2:
time: 752 us; the launch traced here: 739 us
  Pallas kernels  632 us (84%)
  local copies, waits for them, and re-layouts  45.9 us (6%)
  other arithmetic  27.6 us (4%)
  matrix products  18.8 us (2%)
  between operations  14.5 us (2%)
    pallas_call x1, Pallas kernels, run_outputs(): pl.pallas_call(output_kernel, out_shape=[S((4, rows, width), bf16), S((wi...  153 us
    pallas_call x1, Pallas kernels, run_experts(): pl.pallas_call(expert_kernel, out_shape=[jax.ShapeDtypeStruct((rows, widt...  147 us
    pallas_call x1, Pallas kernels, mix_heads(): pl.pallas_call(mix_kernel, out_shape=[S((rows, width), f32), S((rows, wid...  141 us
    pallas_call x1, Pallas kernels, gather_groups(): pl.pallas_call(functools.partial(groups_kernel, parts, count), out_shape=...  103 us
    pallas_call x1, Pallas kernels, pull_inputs(): pl.pallas_call(pull_kernel, out_shape=jax.ShapeDtypeStruct((4, rows + 16,...  33.6 us
    pallas_call x1, Pallas kernels, attend_back(): pl.pallas_call(attend_back_kernel, out_shape=[S((rows, q_width + 2 * HEAD...  33.1 us
    pallas_call x1, Pallas kernels, attend(): pl.pallas_call(attend_kernel, out_shape=[S((rows, width), bf16), S((rows,...  21.6 us
    dot_general x4, matrix products, matmul_tn(): lax.dot_general(left_side, right_side, (((0,), (0,)), ((), ())), preferre...  18.5 us
  transfers between devices with their start and end apart: 3, of which 0 were waited for; matrix products, arithmetic and copies ran while one was open for 8% of the time, Pallas kernels for 52%

profile of v2, /device:TPU:0, one launch (start us, length us, event | category | flops | bytes accessed | tf_op | source)
XLA Modules:
  0.0 738.7 jit_solution(14450280894980045629)
XLA Ops:
  10.3 2.8 concatenate.23
  13.7 2.0 pad_maximum_fusion.refs_1_
  15.7 2.1 dynamic-slice_bitcast_fusion
  17.7 103.4 %shard_map.263 = (bf16[1664,128]{1,0:T(8,128)(2,1)}, bf16[2048,1280]{1,0:T(8,128)(2,1)}, bf16[2048,1024]{1,0:T(8,128)(2,1)}) custom-call(bf16[208,128]{1,0:T(8,128)(2,1)} %pad_bitcast_fusion.refs_0_, bf16[256,1280]{1,0:T(8,128)(2,1)} %pad_maximum_fusion.refs_1_, bf16[256,1024]{1,0:T(8,128)(2,1)} %refs_2_.1), custom_call_target="tpu_custom_call" | custom-call | tf_op jit(solution)/shard_map/pallas_call | solution.py:657
  122.7 4.6 copy.57.gate_ref
  127.4 4.7 copy.58.up_ref
  135.3 21.6 %shard_map.264 = (bf16[512,2048]{1,0:T(8,128)(2,1)S(1)}, f32[512,1152]{1,0:T(8,128)}, bf16[512,1024]{1,0:T(8,128)(2,1)S(1)}, bf16[512,256]{1,0:T(8,128)(2,1)S(1)...) custom-call(bf16[512,2048]{1,0:T(8,128)(2,1)} %bitcast.75, ...), custom_call_target="tpu_custom_call" | custom-call | tf_op jit(solution)/shard_map/pallas_call | solution.py:1169
  158.3 140.8 %shard_map.265 = (f32[128,2048]{1,0:T(8,128)S(1)}, bf16[128,2048]{1,0:T(8,128)(2,1)S(1)}, bf16[4096,2048]{1,0:T(8,128)(2,1)}) custom-call(bf16[512,1024]{1,0:T(8,128)(2,1)S(1)} %get-tuple-element.52.heads_ref, bf16[2048,1024]{1,0:T(8,128)(2,1)S(1)} %copy-done, bf16[128,2048]{1,0:T(8,128)(2,1)S(1)} %get-tuple-element.151.input_ref, f32[1,2048]{1,0:T(1,128)S(1)} %bitcast.80), custom_call_target="tpu_custom_call" | custom-call | tf_op jit(solution)/shard_map/pallas_call | solution.py:602
  303.1 1.4 pad_maximum_fusion.1.router_ref
  304.5 146.7 %shard_map.266 = (f32[128,2048]{1,0:T(8,128)}, bf16[4,144,2176]{2,1,0:T(8,128)(2,1)}, bf16[4096,768]{1,0:T(8,128)(2,1)}, bf16[4096,768]{1,0:T(8,128)(2,1)}, bf16[4096,768]{1,0:T(8,128)(2,1)}) custom-call(bf16[4096,2048]{1,0:T(8,128)(2,1)} %get-tuple-element.54.normed_ref, bf16[4096,2048]{1,0:T(8,128)(2,1)} %all-gather.2.cloned.1.call-done.cot_ref, ...), custom_call_target="tpu_custom_call" | custom-call | tf_op jit(solution)/shard_map/pallas_call | solution.py:1001
  451.2 1.7 slice.84
  454.2 4.5 convolution_convert_fusion.1
  461.0 33.1 %shard_map.267 = (bf16[512,1280]{1,0:T(8,128)(2,1)S(1)}, f32[8,128]{1,0:T(8,128)S(1)}) custom-call(bf16[512,2048]{1,0:T(8,128)(2,1)} %bitcast.86, bf16[2048,1024]{1,0:T(8,128)(2,1)} %get-tuple-element.53.weight_ref.out_w_ref, bf16[512,1024]{1,0:T(8,128)(2,1)S(1)} %get-tuple-element.61.q_ref, bf16[512,256]{1,0:T(8,128)(2,1)S(1)} %copy-done.8, ...), custom_call_target="tpu_custom_call" | custom-call | tf_op jit(solution)/shard_map/pallas_call | solution.py:1248
  494.2 33.6 %shard_map.268 = bf16[4,144,2048]{2,1,0:T(8,128)(2,1)S(1)} custom-call(bf16[512,1280]{1,0:T(8,128)(2,1)S(1)} %get-tuple-element.67.grad_ref, bf16[2048,1280]{1,0:T(8,128)(2,1)S(1)} %bitcast.74, bf16[512,2048]{1,0:T(8,128)(2,1)S(1)} %bitcast.76, f32[1,2048]{1,0:T(1,128)S(1)} %bitcast.79, f32[8,128]{1,0:T(8,128)S(1)} %get-tuple-element.68.head_gain_ref, ...), custom_call_target="tpu_custom_call" | custom-call | tf_op jit(solution)/shard_map/pallas_call | solution.py:747
  528.0 2.7 fusion.3
  531.1 4.9 convolution_convert_fusion
  536.0 6.9 fusion.1
  542.9 152.6 %shard_map.269 = (bf16[4,128,2048]{2,1,0:T(8,128)(2,1)}, f32[2048,768]{1,0:T(8,128)}, f32[2048,768]{1,0:T(8,128)}, f32[768,2048]{1,0:T(8,128)}) custom-call(bf16[4096,2048]{1,0:T(8,128)(2,1)} %get-tuple-element.54.normed_ref, bf16[4096,2048]{1,0:T(8,128)(2,1)} %all-gather.2.cloned.1.call-done.cot_ref, bf16[4096,768]{1,0:T(8,128)(2,1)} %get-tuple-element.71.hid_ref, ...), custom_call_target="tpu_custom_call" | custom-call | tf_op jit(solution)/shard_map/pallas_call | solution.py:1092
  695.6 6.6 copy.60
  702.1 6.7 copy.61
  708.8 2.7 bitcast_convert_fusion
  711.5 1.6 copy-done.15
  713.1 6.4 convolution_add_fusion
  719.5 2.3 convert_element_type.173
  (114 shorter events, 27.8 us)
Async XLA Ops:
  7.2 297.3 %all-gather.2.cloned.1.call-start = ((), (), s32[]{:S(2)}) async-start(), calls=%async_computation.2 | async-start | bytes 17301504 | tf_op jit(solution)/shard_map/all_gather | solution.py:1309
  10.2 112.3 %copy-start.19 = (s32[1,512]{1,0:T(1,128)S(1)}, s32[1,512]{1,0:T(1,128)}, u32[]{:S(2)}) copy-start(s32[1,512]{1,0:T(1,128)} %param.30) | copy-start | bytes 6148
  121.2 598.4 %reduce-scatter.3.cloned.1.call-start = ((), (), s32[]{:S(2)}) async-start(), calls=%async_computation.3 | async-start | bytes 4718592 | tf_op jit(solution)/shard_map/reduce_scatter | solution.py:1401
  132.4 25.9 %copy-start.13 = (f32[1,1,8,256]{3,1,2,0:T(1,128)}, f32[1,1,8,256]{3,1,2,0:T(1,128)S(1)}, u32[]{:S(2)}) copy-start(f32[1,1,8,256]{3,1,2,0:T(1,128)S(1)} %copy.67) | copy-start | bytes 24580
  135.3 23.0 %copy-start = (bf16[2048,1024]{1,0:T(8,128)(2,1)S(1)}, bf16[2048,1024]{1,0:T(8,128)(2,1)}, u32[]{:S(2)}) copy-start(bf16[2048,1024]{1,0:T(8,128)(2,1)} %get-tuple-element.53.weight_ref.out_w_ref) | copy-start | bytes 12582916
  156.9 1.3 copy-start.14
  158.2 140.8 %copy-start.7 = (bf16[512,256]{1,0:T(8,128)(2,1)}, bf16[512,256]{1,0:T(8,128)(2,1)S(1)}, u32[]{:S(2)}) copy-start(bf16[512,256]{1,0:T(8,128)(2,1)S(1)} %get-tuple-element.62.kv_ref) | copy-start | bytes 786436
  158.2 142.6 %copy-start.9 = (bf16[512,256]{1,0:T(8,128)(2,1)}, bf16[512,256]{1,0:T(8,128)(2,1)S(1)}, u32[]{:S(2)}) copy-start(bf16[512,256]{1,0:T(8,128)(2,1)S(1)} %get-tuple-element.63.kv_other_ref) | copy-start | bytes 786436
  158.2 142.6 %copy-start.11 = (f32[512,128]{1,0:T(8,128)}, f32[512,128]{1,0:T(8,128)S(1)}, u32[]{:S(2)}) copy-start(f32[512,128]{1,0:T(8,128)S(1)} %get-tuple-element.66.lse_ref) | copy-start | bytes 786436
  158.2 144.9 %copy-start.17 = (bf16[2048,32]{1,0:T(8,128)(2,1)S(1)}, bf16[2048,32]{1,0:T(8,128)(2,1)}, u32[]{:S(2)}) copy-start(bf16[2048,32]{1,0:T(8,128)(2,1)} %reshape.231) | copy-start | bytes 393220
  452.9 1.3 copy-start.16
  458.8 2.2 copy-start.8
  458.8 2.2 copy-start.10
  458.8 2.2 copy-start.12
  458.8 263.0 %reduce-scatter.5.cloned.1.call-start = ((), (), s32[]{:S(2)}) async-start(), calls=%async_computation.4 | async-start | bytes 6488064 | tf_op jit(solution)/shard_map/reduce_scatter | solution.py:1419
  461.0 33.2 %slice-start = ((s8[5242880]{0:T(1024)(128)(4,1)}), s8[4194304]{0:T(1024)(128)(4,1)S(1)}, s32[]{:S(2)}) async-start(s8[5242880]{0:T(1024)(128)(4,1)} %bitcast.73), calls=%async_computation.5 | async-start | bytes 8388608
  461.0 33.1 %slice-start.1 = ((s8[5242880]{0:T(1024)(128)(4,1)}), s8[1048576]{0:T(1024)(128)(4,1)S(1)}, s32[]{:S(2)}) async-start(s8[5242880]{0:T(1024)(128)(4,1)} %bitcast.73), calls=%async_computation.6 | async-start | bytes 2097152
  461.0 33.1 %copy-start.1 = (bf16[1,512,2048]{2,1,0:T(8,128)(2,1)S(1)}, bf16[1,512,2048]{2,1,0:T(8,128)(2,1)}, u32[]{:S(2)}) copy-start(bf16[1,512,2048]{2,1,0:T(8,128)(2,1)} %param.16) | copy-start | bytes 6291460
  461.0 33.1 %copy-start.5 = (f32[128,2048]{1,0:T(8,128)S(1)}, f32[128,2048]{1,0:T(8,128)}, u32[]{:S(2)}) copy-start(f32[128,2048]{1,0:T(8,128)} %get-tuple-element.69.above_ref) | copy-start | bytes 3145732
  494.1 33.6 %copy-start.4 = (bf16[512,1280]{1,0:T(8,128)(2,1)}, bf16[512,1280]{1,0:T(8,128)(2,1)S(1)}, u32[]{:S(2)}) copy-start(bf16[512,1280]{1,0:T(8,128)(2,1)S(1)} %get-tuple-element.67.grad_ref) | copy-start | bytes 3932164
  527.8 15.2 %copy-start.2 = (bf16[4,144,2048]{2,1,0:T(8,128)(2,1)}, bf16[4,144,2048]{2,1,0:T(8,128)(2,1)S(1)}, u32[]{:S(2)}) copy-start(bf16[4,144,2048]{2,1,0:T(8,128)(2,1)S(1)} %shard_map.268) | copy-start | bytes 7077892
  702.1 6.7 slice-start.2
  708.8 4.3 copy-start.15
  719.5 11.1 %copy-start.18 = (bf16[4,128,2048]{2,1,0:T(8,128)(2,1)S(1)}, bf16[4,128,2048]{2,1,0:T(8,128)(2,1)}, u32[]{:S(2)}) copy-start(bf16[4,128,2048]{2,1,0:T(8,128)(2,1)} %get-tuple-element.74) | copy-start | bytes 6291460
  (2 other events, 1.8 us)
Sparse Core Ops, SparseCore 0:
  121.3 148.6 all-gather.1
  458.9 85.1 reduce-scatter.2
  548.2 144.9 reduce-scatter.4
